TPU v7x, 32 devices: a whole 2x2x4 slice. The times are simulated.
32 devices in a mesh: sec: 8 (over z, x), tile: 4 (over y, core).
Axes of the slice: x: 2, y: 2, z: 4, core: 2. Of those that a mesh axis runs over, the one named last changes fastest.
Arguments:
- features: bfloat16 [8, 2048, 256], P('sec', 'tile'), may hold values from -16 to 16
- select: int32 [8, 2048], P('sec', 'tile'), may hold values from 1 to 7
- validity: int32 [8], P('sec'), may hold values 0 or 1
- offset_gain: float32 [3, 256], replicated, may hold values from 0.5 to 2
Outputs:
- aligned: bfloat16 [8, 2048, 256], P('sec', 'tile')
Inputs may be any that keep to these rules, and one draw needn't show every extreme that they name: `select`: bit k - 1 of a value is 1 where offset k votes.
All inputs are finite; a program needn't handle non-finite values. No bound on the sum of `validity` on one device may be relied on, other than what follows from the above.
Results may differ from a plain program's by a relative error of at most 0.0027.
Values may be sent and summed in bfloat16 or wider, within the bound.
No kernel may reach another device: no remote copies, remote signals or barrier semaphores. Data moves between devices by JAX's collectives and lax.ppermute only.
A program may use at most 64 MiB of HBM per device.

v0:
```python
import math

import jax
import jax.numpy as jnp
from jax import lax
from jax.sharding import PartitionSpec as P

score_factor = 2.5


def from_behind(block, axis, distance):
    devices = range(lax.axis_size(axis))
    route = [(i - distance, i) for i in devices if i - distance in devices]
    return lax.ppermute(block, axis, route)


def make_step(queries, score_scale):

    def fold_step(state_tuple, key_piece, first_row):
        running_max, running_sum, weighted = state_tuple
        key_rows = key_piece[0]
        scores = jnp.dot(queries, key_rows.T, preferred_element_type=jnp.float32) * score_scale
        new_max = jnp.maximum(running_max, jnp.max(scores, axis=1))
        weights = jnp.exp(scores - new_max[:, None])
        running_sum = jnp.sum(weights, axis=1)
        weighted = jnp.dot(
            weights.astype(jnp.bfloat16), key_rows, preferred_element_type=jnp.float32
        )
        return (new_max, running_sum, weighted)

    return fold_step


def shards(features, select, validity, offset_gain):
    queries = features[0]
    num_rows, channels = queries.shape
    fold_step = make_step(queries, score_factor / math.sqrt(channels))
    initial = (
        jnp.full((num_rows,), -1e30, jnp.float32),
        jnp.zeros((num_rows,), jnp.float32),
        jnp.zeros((num_rows, channels), jnp.float32),
    )
    valid_flag = validity.astype(jnp.bfloat16)
    outcomes = []
    received, received_flag = (features, valid_flag)
    for offset in range(1, 4):
        received, received_flag = from_behind((received, received_flag), "sec", 1)
        final_max, final_sum, weighted = fold_step(
            initial, lax.all_gather(received, "tile", axis=1, tiled=True), jnp.int32(0)
        )
        outcomes.append((weighted / final_sum[:, None], received_flag))
    numerator = jnp.zeros((num_rows, channels), jnp.float32)
    vote_count = jnp.zeros((num_rows,), jnp.float32)
    for offset_index in range(3):
        warped, received_flag = outcomes[offset_index]
        chosen = (select[0] // 2**offset_index % 2).astype(jnp.float32) * received_flag.astype(
            jnp.float32
        )[0]
        numerator = numerator + chosen[:, None] * offset_gain[offset_index][None, :] * warped
        vote_count = vote_count + chosen
    aligned = numerator / jnp.maximum(vote_count, 1.0)[:, None]
    return aligned.astype(jnp.bfloat16)[None]


def solution(mesh):
    in_specs = (P("sec", "tile", None), P("sec", "tile"), P("sec"), P())
    out_specs = P("sec", "tile", None)
    return jax.shard_map(shards, mesh=mesh, in_specs=in_specs, out_specs=out_specs, check_vma=False)
```

profile of v0, /device:TPU:0, one launch (start us, length us, event | category | flops | bytes accessed | tf_op | source)
XLA Modules:
  0.0 84.7 jit_solution(6953913337071227885)
XLA Ops:
  6.5 4.9 %collective-permute-start.1 = (bf16[1,512,256]{2,1,0:T(8,128)(2,1)}, bf16[1,512,256]{2,1,0:T(8,128)(2,1)S(1)}, u32[]{:S(2)}, u32[]{:S(2)}) collective-permute-start(bf16[1,512,256]{2,1,0:T(8,128)(2,1)} %param.4), channel_id=1, source_target_pairs={{0,4},{4,8},{8,12},{12,16},{16,20},{20,24},{24,28},{1,5},{5,9},{9,... | collective-permute-start | bytes 786440 | tf_op jit(solution)/shard_map/ppermute | solution.py:14
  11.4 5.8 %collective-permute-done.1 = bf16[1,512,256]{2,1,0:T(8,128)(2,1)S(1)} collective-permute-done((bf16[1,512,256]{2,1,0:T(8,128)(2,1)}, bf16[1,512,256]{2,1,0:T(8,128)(2,1)S(1)}, u32[]{:S(2)}, u32[]{:S(2)}) %collective-permute-start.1) | collective-permute-done | bytes 262176 | tf_op jit(solution)/shard_map/ppermute | solution.py:14
  17.3 0.7 copy-done.5
  18.0 4.3 %collective-permute-start.3 = (bf16[1,512,256]{2,1,0:T(8,128)(2,1)}, bf16[1,512,256]{2,1,0:T(8,128)(2,1)S(1)}, u32[]{:S(2)}, u32[]{:S(2)}) collective-permute-start(bf16[1,512,256]{2,1,0:T(8,128)(2,1)} %copy-done.5), channel_id=1, source_target_pairs={{0,4},{4,8},{8,12},{12,16},{16,20},{20,24},{24,28},{1,5},{5,9},{9,... | collective-permute-start | bytes 786440 | tf_op jit(solution)/shard_map/ppermute | solution.py:14
  22.3 5.0 %collective-permute-done.3 = bf16[1,512,256]{2,1,0:T(8,128)(2,1)S(1)} collective-permute-done((bf16[1,512,256]{2,1,0:T(8,128)(2,1)}, bf16[1,512,256]{2,1,0:T(8,128)(2,1)S(1)}, u32[]{:S(2)}, u32[]{:S(2)}) %collective-permute-start.3) | collective-permute-done | bytes 262176 | tf_op jit(solution)/shard_map/ppermute | solution.py:14
  27.3 0.7 copy-done.4
  28.8 5.6 %collective-permute-start = (bf16[1]{0:T(256)(128)(2,1)}, bf16[1]{0:T(256)(128)(2,1)}, u32[]{:S(2)}, u32[]{:S(2)}) collective-permute-start(bf16[1]{0:T(256)(128)(2,1)} %convert_element_type.49), channel_id=1, source_target_pairs={{0,4},{4,8},{8,12},{12,16},{16,20},{20,24},{24,28},{1,5},{5,9},{9,... | collective-permute-start | bytes 14 | tf_op jit(solution)/shard_map/ppermute | solution.py:14
  34.4 5.2 %collective-permute-start.5 = (bf16[1,512,256]{2,1,0:T(8,128)(2,1)}, bf16[1,512,256]{2,1,0:T(8,128)(2,1)S(1)}, u32[]{:S(2)}, u32[]{:S(2)}) collective-permute-start(bf16[1,512,256]{2,1,0:T(8,128)(2,1)} %copy-done.4), channel_id=1, source_target_pairs={{0,4},{4,8},{8,12},{12,16},{16,20},{20,24},{24,28},{1,5},{5,9},{9,... | collective-permute-start | bytes 786440 | tf_op jit(solution)/shard_map/ppermute | solution.py:14
  39.6 0.8 fusion.84
  41.0 2.5 %collective-permute-start.2 = (bf16[1]{0:T(256)(128)(2,1)}, bf16[1]{0:T(256)(128)(2,1)}, u32[]{:S(2)}, u32[]{:S(2)}) collective-permute-start(bf16[1]{0:T(256)(128)(2,1)} %collective-permute-done), channel_id=1, source_target_pairs={{0,4},{4,8},{8,12},{12,16},{16,20},{20,24},{24,28},{1,5},{5,9},{9,... | collective-permute-start | bytes 14 | tf_op jit(solution)/shard_map/ppermute | solution.py:14
  43.5 0.8 collective-permute-done.2
  45.0 5.5 %collective-permute-start.4 = (bf16[1]{0:T(256)(128)(2,1)}, bf16[1]{0:T(256)(128)(2,1)}, u32[]{:S(2)}, u32[]{:S(2)}) collective-permute-start(bf16[1]{0:T(256)(128)(2,1)} %collective-permute-done.2), channel_id=1, source_target_pairs={{0,4},{4,8},{8,12},{12,16},{16,20},{20,24},{24,28},{1,5},{5,9},{9,... | collective-permute-start | bytes 14 | tf_op jit(solution)/shard_map/ppermute | solution.py:14
  50.5 0.8 collective-permute-done.4
  51.9 0.7 add_maximum_fusion
  53.3 2.2 %multiply_reduce_fusion.2 = (f32[512]{0:T(512)S(1)}, f32[512,2048]{1,0:T(8,128)S(1)}) fusion(bf16[1,2048,256]{2,1,0:T(8,128)(2,1)} %all-gather.4.cloned.1.call-done, bf16[1,512,256]{2,1,0:T(8,128)(2,1)} %param.4), kind=kOutput, calls=%fused_computation.5 | convolution fusion | flops 538967552 | bytes 5507072 | tf_op jit(solution)/shard_map/dot_general | solution.py:22
  55.6 0.8 fusion
  56.4 0.8 %fusion.21 = f32[512,256]{1,0:T(8,128)S(1)} fusion(f32[512,2048]{1,0:T(8,128)S(1)} %get-tuple-element.13, f32[512]{0:T(512)S(1)} %broadcast_maximum_fusion.2, bf16[1,2048,256]{2,1,0:T(8,128)(2,1)S(1)} %copy-done.2, f32[512]{0:T(512)S(1)} %fusion, f32[256]{0:T(256)S(1)} %bitcast.55, f32[512]{0:T(512)S(1)} %get-tuple-element.8), kind=kOutput, calls=%fused_computation.22 | convolution fusion | flops 540409856 | bytes 5774336 | tf_op jit(solution)/shard_map/dot_general | solution.py:26
  57.4 2.1 %multiply_reduce_fusion.1 = (f32[512]{0:T(512)S(1)}, f32[512,2048]{1,0:T(8,128)S(1)}) fusion(bf16[1,2048,256]{2,1,0:T(8,128)(2,1)} %all-gather.6.cloned.1.call-done, bf16[1,512,256]{2,1,0:T(8,128)(2,1)S(1)} %copy-done), kind=kOutput, calls=%fused_computation.4 | convolution fusion | flops 538967552 | bytes 5507072 | tf_op jit(solution)/shard_map/dot_general | solution.py:22
  59.5 0.8 fusion.2
  60.3 0.9 %fusion.30 = f32[512,256]{1,0:T(8,128)S(1)} fusion(f32[512,256]{1,0:T(8,128)S(1)} %fusion.21, f32[512,2048]{1,0:T(8,128)S(1)} %get-tuple-element.15, f32[512]{0:T(512)S(1)} %broadcast_maximum_fusion.1, bf16[1,2048,256]{2,1,0:T(8,128)(2,1)S(1)} %copy-done.1, f32[512]{0:T(512)S(1)} %fusion.2, f32[256]{0:T(256)S(1)} %bitcast.54, f32[512]{0:T(512)S(1)} %get-tuple-element.7), kind=kOutput, calls=%fused_computation.25 | convolution fusion | flops 540540928 | bytes 6298624 | tf_op jit(solution)/shard_map/dot_general | solution.py:26
  61.2 12.4 %all-gather.8.cloned.1.call-done = bf16[1,2048,256]{2,1,0:T(8,128)(2,1)} async-done(((bf16[1,512,256]{2,1,0:T(8,128)(2,1)}), bf16[1,2048,256]{2,1,0:T(8,128)(2,1)}) %all-gather.8.cloned.1.call-update) | async-done | bytes 1048592 | tf_op jit(solution)/shard_map/all_gather | solution.py:49
  73.6 2.1 %multiply_reduce_fusion = (f32[512]{0:T(512)S(1)}, f32[512,2048]{1,0:T(8,128)S(1)}) fusion(bf16[1,2048,256]{2,1,0:T(8,128)(2,1)} %all-gather.8.cloned.1.call-done, bf16[1,512,256]{2,1,0:T(8,128)(2,1)S(1)} %copy-done), kind=kOutput, calls=%fused_computation.3 | convolution fusion | flops 538967552 | bytes 5507072 | tf_op jit(solution)/shard_map/dot_general | solution.py:22
  75.7 0.8 fusion.4
  76.6 1.6 %fusion.61 = bf16[1,512,256]{2,1,0:T(8,128)(2,1)} fusion(f32[512,256]{1,0:T(8,128)S(1)} %fusion.30, bf16[1,2048,256]{2,1,0:T(8,128)(2,1)S(1)} %copy-done.3, f32[512,2048]{1,0:T(8,128)S(1)} %get-tuple-element.17, f32[512]{0:T(512)S(1)} %broadcast_maximum_fusion, f32[512]{0:T(512)S(1)} %get-tuple-element.5, f32[512]{0:T(512)S(1)} %fusion.4, ...), kind=kOutput, calls=%fused_computation.40 | convolution fusion | flops 540803072 | bytes 6038528 | tf_op jit(solution)/shard_map/dot_general | solution.py:26
  (25 shorter events, 1.0 us)
Async XLA Ops:
  6.5 46.8 %all-gather.4.cloned.1.call-start = ((), (), s32[]{:S(2)}) async-start(), calls=%async_computation | async-start | bytes 1310720 | tf_op jit(solution)/shard_map/all_gather | solution.py:49
  6.5 10.7 %collective-permute-start.1 = (bf16[1,512,256]{2,1,0:T(8,128)(2,1)}, bf16[1,512,256]{2,1,0:T(8,128)(2,1)S(1)}, u32[]{:S(2)}, u32[]{:S(2)}) collective-permute-start(bf16[1,512,256]{2,1,0:T(8,128)(2,1)} %param.4), channel_id=1, source_target_pairs={{0,4},{4,8},{8,12},{12,16},{16,20},{20,24},{24,28},{1,5},{5,9},{9,... | collective-permute-start | bytes 786440 | tf_op jit(solution)/shard_map/ppermute | solution.py:14
  17.3 0.7 copy-start.5
  18.0 39.3 %all-gather.6.cloned.1.call-start = ((), (), s32[]{:S(2)}) async-start(), calls=%async_computation.1 | async-start | bytes 1310720 | tf_op jit(solution)/shard_map/all_gather | solution.py:49
  18.0 9.3 %collective-permute-start.3 = (bf16[1,512,256]{2,1,0:T(8,128)(2,1)}, bf16[1,512,256]{2,1,0:T(8,128)(2,1)S(1)}, u32[]{:S(2)}, u32[]{:S(2)}) collective-permute-start(bf16[1,512,256]{2,1,0:T(8,128)(2,1)} %copy-done.5), channel_id=1, source_target_pairs={{0,4},{4,8},{8,12},{12,16},{16,20},{20,24},{24,28},{1,5},{5,9},{9,... | collective-permute-start | bytes 786440 | tf_op jit(solution)/shard_map/ppermute | solution.py:14
  27.3 0.7 copy-start.4
  28.1 45.5 %all-gather.8.cloned.1.call-start = ((), (), s32[]{:S(2)}) async-start(), calls=%async_computation.2 | async-start | bytes 1310720 | tf_op jit(solution)/shard_map/all_gather | solution.py:49
  28.8 11.6 %collective-permute-start = (bf16[1]{0:T(256)(128)(2,1)}, bf16[1]{0:T(256)(128)(2,1)}, u32[]{:S(2)}, u32[]{:S(2)}) collective-permute-start(bf16[1]{0:T(256)(128)(2,1)} %convert_element_type.49), channel_id=1, source_target_pairs={{0,4},{4,8},{8,12},{12,16},{16,20},{20,24},{24,28},{1,5},{5,9},{9,... | collective-permute-start | bytes 14 | tf_op jit(solution)/shard_map/ppermute | solution.py:14
  34.4 18.2 %collective-permute-start.5 = (bf16[1,512,256]{2,1,0:T(8,128)(2,1)}, bf16[1,512,256]{2,1,0:T(8,128)(2,1)S(1)}, u32[]{:S(2)}, u32[]{:S(2)}) collective-permute-start(bf16[1,512,256]{2,1,0:T(8,128)(2,1)} %copy-done.4), channel_id=1, source_target_pairs={{0,4},{4,8},{8,12},{12,16},{16,20},{20,24},{24,28},{1,5},{5,9},{9,... | collective-permute-start | bytes 786440 | tf_op jit(solution)/shard_map/ppermute | solution.py:14
  41.0 3.2 %collective-permute-start.2 = (bf16[1]{0:T(256)(128)(2,1)}, bf16[1]{0:T(256)(128)(2,1)}, u32[]{:S(2)}, u32[]{:S(2)}) collective-permute-start(bf16[1]{0:T(256)(128)(2,1)} %collective-permute-done), channel_id=1, source_target_pairs={{0,4},{4,8},{8,12},{12,16},{16,20},{20,24},{24,28},{1,5},{5,9},{9,... | collective-permute-start | bytes 14 | tf_op jit(solution)/shard_map/ppermute | solution.py:14
  45.0 6.3 %collective-permute-start.4 = (bf16[1]{0:T(256)(128)(2,1)}, bf16[1]{0:T(256)(128)(2,1)}, u32[]{:S(2)}, u32[]{:S(2)}) collective-permute-start(bf16[1]{0:T(256)(128)(2,1)} %collective-permute-done.2), channel_id=1, source_target_pairs={{0,4},{4,8},{8,12},{12,16},{16,20},{20,24},{24,28},{1,5},{5,9},{9,... | collective-permute-start | bytes 14 | tf_op jit(solution)/shard_map/ppermute | solution.py:14
  52.6 0.7 copy-start.6
  53.3 3.1 %copy-start.2 = (bf16[1,2048,256]{2,1,0:T(8,128)(2,1)S(1)}, bf16[1,2048,256]{2,1,0:T(8,128)(2,1)}, u32[]{:S(2)}) copy-start(bf16[1,2048,256]{2,1,0:T(8,128)(2,1)} %all-gather.4.cloned.1.call-done) | copy-start | bytes 3145732
  56.4 1.0 %copy-start = (bf16[1,512,256]{2,1,0:T(8,128)(2,1)S(1)}, bf16[1,512,256]{2,1,0:T(8,128)(2,1)}, u32[]{:S(2)}) copy-start(bf16[1,512,256]{2,1,0:T(8,128)(2,1)} %param.4) | copy-start | bytes 786436
  57.4 3.0 %copy-start.1 = (bf16[1,2048,256]{2,1,0:T(8,128)(2,1)S(1)}, bf16[1,2048,256]{2,1,0:T(8,128)(2,1)}, u32[]{:S(2)}) copy-start(bf16[1,2048,256]{2,1,0:T(8,128)(2,1)} %all-gather.6.cloned.1.call-done) | copy-start | bytes 3145732
  73.6 3.0 %copy-start.3 = (bf16[1,2048,256]{2,1,0:T(8,128)(2,1)S(1)}, bf16[1,2048,256]{2,1,0:T(8,128)(2,1)}, u32[]{:S(2)}) copy-start(bf16[1,2048,256]{2,1,0:T(8,128)(2,1)} %all-gather.8.cloned.1.call-done) | copy-start | bytes 3145732
Sparse Core Ops, SparseCore 0:
  18.1 18.8 all-gather.3
  38.5 16.6 all-gather.5
  56.8 16.6 all-gather.7
where the time goes:
time: 85.1 us; the launch traced here: 84.7 us
  starting transfers between devices  28.1 us (33%)
  waiting for transfers between devices  24.9 us (29%)
  between operations  15.8 us (19%)
  matrix products  9.81 us (12%)
  other arithmetic  3.2 us (4%)
  local copies, waits for them, and re-layouts  2.96 us (3%)
    ppermute x6, starting transfers between devices, from_behind(): return lax.ppermute(block, axis, route)  28 us
    all_gather x3, waiting for transfers between devices, shards(): lax.all_gather(received, 'tile', axis=1, tiled=True)  12.4 us
    ppermute x6, waiting for transfers between devices, from_behind(): return lax.ppermute(block, axis, route)  12.4 us
    dot_general x3, matrix products, fold_step(): jnp.dot(queries, key_rows.T, preferred_element_type=jnp.float32)  6.5 us
    dot_general x3, matrix products, fold_step(): jnp.dot(weights.astype(jnp.bfloat16), key_rows, preferred_element_type=jn...  3.32 us
    reduce_sum x3, other arithmetic, fold_step(): running_sum = jnp.sum(weights, axis=1)  2.47 us
    unnamed x14, local copies, waits for them, and re-layouts  2.16 us
  transfers between devices with their start and end apart: 9, of which 5 were waited for; matrix products, arithmetic and copies ran while one was open for 11% of the time, Pallas kernels for 0%

commit v1 on v0

v1 whole, which is shorter than its diff:
```python
import functools
import math

import jax
import jax.numpy as jnp
from jax import lax
from jax.experimental import pallas as pl
from jax.experimental.pallas import tpu as pltpu
from jax.sharding import PartitionSpec as P

score_factor = 2.5
offsets = 3
unusable = 32.0
usable_limit = 16.0
lanes = 128
row_block = 256
vmem = pl.BlockSpec(memory_space=pltpu.VMEM)
grant = pltpu.CompilerParams(vmem_limit_bytes=24 * 2**20)
smem = pl.BlockSpec(memory_space=pltpu.SMEM)


def from_behind(block, distance):
    n = lax.axis_size("sec")
    return lax.ppermute(block, "sec", [((i - distance) % n, i) for i in range(n)])


def from_partner(block, distance):
    return lax.ppermute(block, "tile", [(i ^ distance, i) for i in range(lax.axis_size("tile"))])


def prepare(select_ref, columns_ref):
    rows = jnp.broadcast_to(select_ref[...].astype(jnp.float32), (lanes, select_ref.shape[1]))
    columns_ref[...] = rows.T.astype(jnp.int32)


def fold(offset, first, last, scale, *refs):
    section_ref, query_ref, columns_ref, gain_ref, *refs = refs
    if not first:
        numerator_ref, count_ref, *refs = refs
    *key_refs, out_ref = refs[: len(refs) if last else -1]
    count_out_ref = None if last else refs[-1]
    num_rows, channels = query_ref.shape
    step = scale * math.log2(math.e)
    mark = key_refs[0][0:8, 0:lanes].astype(jnp.float32)[0:1, :]
    behind = (section_ref[0] >= offset).astype(jnp.float32)
    usable = jnp.where(mark <= usable_limit, behind, 0.0)
    gain = gain_ref[offset - 1 : offset, :]
    for row in range(0, num_rows, row_block):
        rows = slice(row, row + row_block)
        queries = query_ref[rows, :]
        scores = [
            lax.dot_general(
                queries, k[...], (((1,), (1,)), ((), ())), preferred_element_type=jnp.float32
            )
            for k in key_refs
        ]
        top = functools.reduce(jnp.maximum, [s.max(axis=1, keepdims=True) for s in scores]) * step
        total = 0.0
        weighted = 0.0
        for s, k in zip(scores, key_refs):
            weights = jnp.exp2(s * step - top)
            total = total + jnp.sum(weights, axis=1, keepdims=True)
            weighted = weighted + jnp.dot(
                weights.astype(jnp.bfloat16), k[...], preferred_element_type=jnp.float32
            )
        bits = (columns_ref[rows, :] >> (offset - 1)) & 1
        chosen = bits.astype(jnp.float32) * usable
        share = jnp.concatenate([chosen / total] * (channels // lanes), axis=1)
        numerator = weighted * share * gain
        count = chosen
        if not first:
            numerator = numerator + numerator_ref[rows, :]
            count = count + count_ref[rows, :]
        if last:
            divisor = jnp.concatenate([jnp.maximum(count, 1.0)] * (channels // lanes), axis=1)
            out_ref[rows, :] = (numerator / divisor).astype(jnp.bfloat16)
        else:
            out_ref[rows, :] = numerator
            count_out_ref[rows, :] = count


def shards(features, select, validity, offset_gain):
    queries = features[0]
    num_rows, channels = queries.shape
    scale = score_factor / math.sqrt(channels)
    section = lax.axis_index("sec").astype(jnp.int32)[None]
    columns = pl.pallas_call(
        prepare,
        out_shape=jax.ShapeDtypeStruct((num_rows, lanes), jnp.int32),
        in_specs=[vmem],
        out_specs=vmem,
        compiler_params=grant,
        name="prepare",
    )(select)
    sent = jnp.where(validity[0] != 0, queries, jnp.bfloat16(unusable))
    second = from_behind(sent, 2)
    first = from_behind(sent, 1)
    third = from_behind(second, 1)

    def all_tiles(tile):
        tiles = [tile]
        distance = lax.axis_size("tile") // 2
        while distance:
            tiles += [from_partner(t, distance) for t in tiles]
            distance //= 2
        return tiles

    state = []
    order = [(2, second), (1, first), (3, third)]
    for at, (offset, tile) in enumerate(order):
        last = at == len(order) - 1
        tiles = all_tiles(tile)
        keys = len(tiles) * num_rows
        wide = jax.ShapeDtypeStruct((num_rows, channels), jnp.bfloat16 if last else jnp.float32)
        narrow = jax.ShapeDtypeStruct((num_rows, lanes), jnp.float32)
        args = (section, queries, columns, offset_gain, *state, *tiles)
        state = pl.pallas_call(
            functools.partial(fold, offset, at == 0, last, scale),
            out_shape=wide if last else (wide, narrow),
            in_specs=[smem] + [vmem] * (len(args) - 1),
            out_specs=vmem if last else (vmem, vmem),
            cost_estimate=pl.CostEstimate(
                flops=4 * num_rows * keys * channels,
                transcendentals=num_rows * keys,
                bytes_accessed=2 * keys * channels,
            ),
            compiler_params=grant,
            name=f"fold{offset}",
        )(*args)
    return state[None]


def solution(mesh):
    in_specs = (P("sec", "tile", None), P("sec", "tile"), P("sec"), P())
    out_specs = P("sec", "tile", None)
    return jax.shard_map(shards, mesh=mesh, in_specs=in_specs, out_specs=out_specs, check_vma=False)
```

time: 85.1 us -> 42.6 us (0.50)
  starting transfers between devices: 28.1 us -> 12.7 us
  between operations: 15.8 us -> 0.77 us
  matrix products: 9.81 us -> 0 us
  Pallas kernels: 0 us -> 8.36 us
  waiting for transfers between devices: 24.9 us -> 18.9 us
  local copies, waits for them, and re-layouts: 2.96 us -> 0.67 us
  other arithmetic: 3.2 us -> 0.98 us
    ppermute x6 -> x12, starting transfers between devices: 28 us -> 12.7 us  [the longest x3 7.16 us: from_behind(): lax.ppermute(block, 'sec', [((i - distance) % n, i) for i in range(n)])]
    all_gather x3 -> x0, waiting for transfers between devices: 12.4 us -> none  [shards(): lax.all_gather(received, 'tile', axis=1, tiled=True)]
    dot_general x6 -> x0, matrix products: 9.81 us -> none  [the longest x3 6.5 us: fold_step(): jnp.dot(queries, key_rows.T, preferred_element_type=jnp.float32)]
    pallas_call x0 -> x4, Pallas kernels: none -> 8.36 us  [the longest x3 8.22 us: shards(): pl.pallas_call(functools.partial(fold, offset, at == 0, last, scale), out...]
    ppermute x6 -> x12, waiting for transfers between devices: 12.4 us -> 18.9 us  [the longest x3 13.4 us: from_behind(): lax.ppermute(block, 'sec', [((i - distance) % n, i) for i in range(n)])]
    reduce_sum x3 -> x0, other arithmetic: 2.47 us -> none  [fold_step(): running_sum = jnp.sum(weights, axis=1)]
    unnamed x14 -> x6, local copies, waits for them, and re-layouts: 2.16 us -> 0.67 us
    select_n x0 -> x1, other arithmetic: none -> 0.98 us  [shards(): sent = jnp.where(validity[0] != 0, queries, jnp.bfloat16(unusable))]
  transfers between devices with their start and end apart: 9 -> 12, of which waited for: 5 -> 5; matrix products, arithmetic and copies ran while one was open for 11% -> 0% of each run, Pallas kernels for 0% -> 13%
where the time goes in v1:
time: 42.6 us; the launch traced here: 42.4 us
  waiting for transfers between devices  18.9 us (44%)
  starting transfers between devices  12.7 us (30%)
  Pallas kernels  8.36 us (20%)
  other arithmetic  0.98 us (2%)
  between operations  0.77 us (2%)
  local copies, waits for them, and re-layouts  0.67 us (2%)
    ppermute x3, waiting for transfers between devices, from_behind(): lax.ppermute(block, 'sec', [((i - distance) % n, i) for i in range(n)])  13.4 us
    pallas_call x3, Pallas kernels, shards(): pl.pallas_call(functools.partial(fold, offset, at == 0, last, scale), out...  8.22 us
    ppermute x3, starting transfers between devices, from_behind(): lax.ppermute(block, 'sec', [((i - distance) % n, i) for i in range(n)])  7.16 us
    ppermute x9, starting transfers between devices, from_partner(): lax.ppermute(block, 'tile', [(i ^ distance, i) for i in range(lax.axis_si...  5.58 us
    ppermute x9, waiting for transfers between devices, from_partner(): lax.ppermute(block, 'tile', [(i ^ distance, i) for i in range(lax.axis_si...  5.48 us
    select_n x1, other arithmetic, shards(): sent = jnp.where(validity[0] != 0, queries, jnp.bfloat16(unusable))  0.98 us
  transfers between devices with their start and end apart: 12, of which 5 were waited for; matrix products, arithmetic and copies ran while one was open for 0% of the time, Pallas kernels for 13%

profile of v1, /device:TPU:0, one launch (start us, length us, event | category | flops | bytes accessed | tf_op | source)
XLA Modules:
  0.0 42.4 jit_solution(4196713621939413756)
XLA Ops:
  0.7 1.0 %broadcast_select_fusion = bf16[512,256]{1,0:T(8,128)(2,1)S(1)} fusion(pred[]{:T(512)} %bitcast.2, bf16[1,512,256]{2,1,0:T(8,128)(2,1)} %param.4), kind=kLoop, calls=%fused_computation | loop fusion | flops 131072 | bytes 524289 | tf_op jit(solution)/shard_map/jit(_where)/select_n | solution.py:95
  1.6 0.0 copy-start
  1.7 3.1 %collective-permute-start = (bf16[512,256]{1,0:T(8,128)(2,1)S(1)}, bf16[512,256]{1,0:T(8,128)(2,1)S(1)}, u32[]{:S(2)}, u32[]{:S(2)}) collective-permute-start(bf16[512,256]{1,0:T(8,128)(2,1)S(1)} %broadcast_select_fusion), channel_id=1, source_target_pairs={{24,0},{28,4},{0,8},{4,12},{8,16},{12,20},{16,24},{20,28},{25,1},{... | collective-permute-start | bytes 786440 | tf_op jit(solution)/shard_map/ppermute | solution.py:24
  4.8 1.5 %collective-permute-start.4 = (bf16[512,256]{1,0:T(8,128)(2,1)S(1)}, bf16[512,256]{1,0:T(8,128)(2,1)S(1)}, u32[]{:S(2)}, u32[]{:S(2)}) collective-permute-start(bf16[512,256]{1,0:T(8,128)(2,1)S(1)} %broadcast_select_fusion), channel_id=1, source_target_pairs={{28,0},{0,4},{4,8},{8,12},{12,16},{16,20},{20,24},{24,28},{29,1},{... | collective-permute-start | bytes 786440 | tf_op jit(solution)/shard_map/ppermute | solution.py:24
  6.3 6.8 %collective-permute-done.refs_4_ = bf16[512,256]{1,0:T(8,128)(2,1)S(1)} collective-permute-done((bf16[512,256]{1,0:T(8,128)(2,1)S(1)}, bf16[512,256]{1,0:T(8,128)(2,1)S(1)}, u32[]{:S(2)}, u32[]{:S(2)}) %collective-permute-start) | collective-permute-done | bytes 262176 | tf_op jit(solution)/shard_map/ppermute | solution.py:24
  13.1 2.6 %collective-permute-start.8 = (bf16[512,256]{1,0:T(8,128)(2,1)S(1)}, bf16[512,256]{1,0:T(8,128)(2,1)S(1)}, u32[]{:S(2)}, u32[]{:S(2)}) collective-permute-start(bf16[512,256]{1,0:T(8,128)(2,1)S(1)} %collective-permute-done.refs_4_), channel_id=1, source_target_pairs={{28,0},{0,4},{4,8},{8,12},{12,16},{16,20},{20,24},{24,28},{29,1},{... | collective-permute-start | bytes 786440 | tf_op jit(solution)/shard_map/ppermute | solution.py:24
  15.7 1.5 %collective-permute-start.1 = (bf16[512,256]{1,0:T(8,128)(2,1)S(1)}, bf16[512,256]{1,0:T(8,128)(2,1)S(1)}, u32[]{:S(2)}, u32[]{:S(2)}) collective-permute-start(bf16[512,256]{1,0:T(8,128)(2,1)S(1)} %collective-permute-done.refs_4_), channel_id=1, source_target_pairs={{2,0},{3,1},{0,2},{1,3},{6,4},{7,5},{4,6},{5,7},{10,8},{11,9},{8,1... | collective-permute-start | bytes 786440 | tf_op jit(solution)/shard_map/ppermute | solution.py:28
  17.2 3.5 %collective-permute-done.4.refs_6_ = bf16[512,256]{1,0:T(8,128)(2,1)S(1)} collective-permute-done((bf16[512,256]{1,0:T(8,128)(2,1)S(1)}, bf16[512,256]{1,0:T(8,128)(2,1)S(1)}, u32[]{:S(2)}, u32[]{:S(2)}) %collective-permute-start.4) | collective-permute-done | bytes 262176 | tf_op jit(solution)/shard_map/ppermute | solution.py:24
  20.7 1.5 %collective-permute-start.5 = (bf16[512,256]{1,0:T(8,128)(2,1)S(1)}, bf16[512,256]{1,0:T(8,128)(2,1)S(1)}, u32[]{:S(2)}, u32[]{:S(2)}) collective-permute-start(bf16[512,256]{1,0:T(8,128)(2,1)S(1)} %collective-permute-done.4.refs_6_), channel_id=1, source_target_pairs={{2,0},{3,1},{0,2},{1,3},{6,4},{7,5},{4,6},{5,7},{10,8},{11,9},{8,1... | collective-permute-start | bytes 786440 | tf_op jit(solution)/shard_map/ppermute | solution.py:28
  22.2 3.0 %collective-permute-done.8.refs_6_ = bf16[512,256]{1,0:T(8,128)(2,1)S(1)} collective-permute-done((bf16[512,256]{1,0:T(8,128)(2,1)S(1)}, bf16[512,256]{1,0:T(8,128)(2,1)S(1)}, u32[]{:S(2)}, u32[]{:S(2)}) %collective-permute-start.8) | collective-permute-done | bytes 262176 | tf_op jit(solution)/shard_map/ppermute | solution.py:24
  25.3 1.5 %collective-permute-start.9 = (bf16[512,256]{1,0:T(8,128)(2,1)S(1)}, bf16[512,256]{1,0:T(8,128)(2,1)S(1)}, u32[]{:S(2)}, u32[]{:S(2)}) collective-permute-start(bf16[512,256]{1,0:T(8,128)(2,1)S(1)} %collective-permute-done.8.refs_6_), channel_id=1, source_target_pairs={{2,0},{3,1},{0,2},{1,3},{6,4},{7,5},{4,6},{5,7},{10,8},{11,9},{8,1... | collective-permute-start | bytes 786440 | tf_op jit(solution)/shard_map/ppermute | solution.py:28
  26.8 0.0 collective-permute-done.1.refs_5_
  26.8 0.0 collective-permute-start.3
  26.8 0.5 %collective-permute-start.6 = (bf16[512,256]{1,0:T(8,128)(2,1)S(1)}, bf16[512,256]{1,0:T(8,128)(2,1)S(1)}, u32[]{:S(2)}, u32[]{:S(2)}) collective-permute-start(bf16[512,256]{1,0:T(8,128)(2,1)S(1)} %collective-permute-done.4.refs_6_), channel_id=1, source_target_pairs={{1,0},{0,1},{3,2},{2,3},{5,4},{4,5},{7,6},{6,7},{9,8},{8,9},{11,10... | collective-permute-start | bytes 786440 | tf_op jit(solution)/shard_map/ppermute | solution.py:28
  27.3 1.1 %collective-permute-done.5.refs_7_ = bf16[512,256]{1,0:T(8,128)(2,1)S(1)} collective-permute-done((bf16[512,256]{1,0:T(8,128)(2,1)S(1)}, bf16[512,256]{1,0:T(8,128)(2,1)S(1)}, u32[]{:S(2)}, u32[]{:S(2)}) %collective-permute-start.5) | collective-permute-done | bytes 262176 | tf_op jit(solution)/shard_map/ppermute | solution.py:28
  28.4 0.0 collective-permute-start.7
  28.4 0.5 %collective-permute-start.10 = (bf16[512,256]{1,0:T(8,128)(2,1)S(1)}, bf16[512,256]{1,0:T(8,128)(2,1)S(1)}, u32[]{:S(2)}, u32[]{:S(2)}) collective-permute-start(bf16[512,256]{1,0:T(8,128)(2,1)S(1)} %collective-permute-done.8.refs_6_), channel_id=1, source_target_pairs={{1,0},{0,1},{3,2},{2,3},{5,4},{4,5},{7,6},{6,7},{9,8},{8,9},{11,10... | collective-permute-start | bytes 786440 | tf_op jit(solution)/shard_map/ppermute | solution.py:28
  28.9 4.4 %collective-permute-done.9.refs_7_ = bf16[512,256]{1,0:T(8,128)(2,1)S(1)} collective-permute-done((bf16[512,256]{1,0:T(8,128)(2,1)S(1)}, bf16[512,256]{1,0:T(8,128)(2,1)S(1)}, u32[]{:S(2)}, u32[]{:S(2)}) %collective-permute-start.9) | collective-permute-done | bytes 262176 | tf_op jit(solution)/shard_map/ppermute | solution.py:28
  33.3 0.1 prepare.1.refs_2_
  33.4 0.0 copy-start.2
  33.4 0.7 %copy-done.2 = f32[3,256]{1,0:T(4,128)S(1)} copy-done((f32[3,256]{1,0:T(4,128)S(1)}, f32[3,256]{1,0:T(4,128)}, u32[]{:S(2)}) %copy-start.2) | copy-done | bytes 3096
  34.1 3.1 %fold2.1 = (f32[512,256]{1,0:T(8,128)S(1)}, f32[512,128]{1,0:T(8,128)S(1)}) custom-call(s32[1]{0:T(128)} %bitcast.refs_0_, bf16[512,256]{1,0:T(8,128)(2,1)S(1)} %bitcast.5, s32[512,128]{1,0:T(8,128)S(1)} %prepare.1.refs_2_, f32[3,256]{1,0:T(4,128)S(1)} %copy-done.2, bf16[512,256]{1,0:T(8,128)(2,1)S(1)} %collective-permute-done.refs_4_, ...), custom_call_target="tpu_custom_call" | custom-call | flops 1073741824 | bytes 1048576 | tf_op jit(solution)/shard_map/fold2/pallas_call | solution.py:117
  37.2 2.2 %fold1.1 = (f32[512,256]{1,0:T(8,128)S(1)}, f32[512,128]{1,0:T(8,128)S(1)}) custom-call(s32[1]{0:T(128)} %bitcast.refs_0_, bf16[512,256]{1,0:T(8,128)(2,1)S(1)} %bitcast.6, s32[512,128]{1,0:T(8,128)S(1)} %prepare.1.refs_2_, f32[3,256]{1,0:T(4,128)S(1)} %copy-done.2, f32[512,256]{1,0:T(8,128)S(1)} %get-tuple-element.9.refs_4_, ...), custom_call_target="tpu_custom_call" | custom-call | flops 1073741824 | bytes 1048576 | tf_op jit(solution)/shard_map/fold1/pallas_call | solution.py:117
  39.5 2.9 %fold3.1 = bf16[512,256]{1,0:T(8,128)(2,1)} custom-call(s32[1]{0:T(128)} %bitcast.refs_0_, bf16[512,256]{1,0:T(8,128)(2,1)S(1)} %bitcast.7, s32[512,128]{1,0:T(8,128)S(1)} %prepare.1.refs_2_, f32[3,256]{1,0:T(4,128)S(1)} %copy-done.2, f32[512,256]{1,0:T(8,128)S(1)} %get-tuple-element.11.refs_4_, f32[512,128]{1,0:T(8,128)S(1)} %get-tuple-element.12.refs_5_, ...), custom_call_target="tpu_custom_call" | custom-call | flops 1073741824 | bytes 1048576 | tf_op jit(solution)/shard_map/fold3/pallas_call | solution.py:117
  (11 shorter events, 0.0 us)
Async XLA Ops:
  0.7 32.6 %copy-start.1 = (s32[1,512]{1,0:T(1,128)S(1)}, s32[1,512]{1,0:T(1,128)}, u32[]{:S(2)}) copy-start(s32[1,512]{1,0:T(1,128)} %select_ref.1) | copy-start | bytes 6148
  1.6 31.8 %copy-start = (bf16[1,512,256]{2,1,0:T(8,128)(2,1)S(1)}, bf16[1,512,256]{2,1,0:T(8,128)(2,1)}, u32[]{:S(2)}) copy-start(bf16[1,512,256]{2,1,0:T(8,128)(2,1)} %param.4) | copy-start | bytes 786436
  1.7 11.4 %collective-permute-start = (bf16[512,256]{1,0:T(8,128)(2,1)S(1)}, bf16[512,256]{1,0:T(8,128)(2,1)S(1)}, u32[]{:S(2)}, u32[]{:S(2)}) collective-permute-start(bf16[512,256]{1,0:T(8,128)(2,1)S(1)} %broadcast_select_fusion), channel_id=1, source_target_pairs={{24,0},{28,4},{0,8},{4,12},{8,16},{12,20},{16,24},{20,28},{25,1},{... | collective-permute-start | bytes 786440 | tf_op jit(solution)/shard_map/ppermute | solution.py:24
  4.8 15.9 %collective-permute-start.4 = (bf16[512,256]{1,0:T(8,128)(2,1)S(1)}, bf16[512,256]{1,0:T(8,128)(2,1)S(1)}, u32[]{:S(2)}, u32[]{:S(2)}) collective-permute-start(bf16[512,256]{1,0:T(8,128)(2,1)S(1)} %broadcast_select_fusion), channel_id=1, source_target_pairs={{28,0},{0,4},{4,8},{8,12},{12,16},{16,20},{20,24},{24,28},{29,1},{... | collective-permute-start | bytes 786440 | tf_op jit(solution)/shard_map/ppermute | solution.py:24
  13.1 12.2 %collective-permute-start.8 = (bf16[512,256]{1,0:T(8,128)(2,1)S(1)}, bf16[512,256]{1,0:T(8,128)(2,1)S(1)}, u32[]{:S(2)}, u32[]{:S(2)}) collective-permute-start(bf16[512,256]{1,0:T(8,128)(2,1)S(1)} %collective-permute-done.refs_4_), channel_id=1, source_target_pairs={{28,0},{0,4},{4,8},{8,12},{12,16},{16,20},{20,24},{24,28},{29,1},{... | collective-permute-start | bytes 786440 | tf_op jit(solution)/shard_map/ppermute | solution.py:24
  15.7 11.1 %collective-permute-start.1 = (bf16[512,256]{1,0:T(8,128)(2,1)S(1)}, bf16[512,256]{1,0:T(8,128)(2,1)S(1)}, u32[]{:S(2)}, u32[]{:S(2)}) collective-permute-start(bf16[512,256]{1,0:T(8,128)(2,1)S(1)} %collective-permute-done.refs_4_), channel_id=1, source_target_pairs={{2,0},{3,1},{0,2},{1,3},{6,4},{7,5},{4,6},{5,7},{10,8},{11,9},{8,1... | collective-permute-start | bytes 786440 | tf_op jit(solution)/shard_map/ppermute | solution.py:28
  20.7 7.7 %collective-permute-start.5 = (bf16[512,256]{1,0:T(8,128)(2,1)S(1)}, bf16[512,256]{1,0:T(8,128)(2,1)S(1)}, u32[]{:S(2)}, u32[]{:S(2)}) collective-permute-start(bf16[512,256]{1,0:T(8,128)(2,1)S(1)} %collective-permute-done.4.refs_6_), channel_id=1, source_target_pairs={{2,0},{3,1},{0,2},{1,3},{6,4},{7,5},{4,6},{5,7},{10,8},{11,9},{8,1... | collective-permute-start | bytes 786440 | tf_op jit(solution)/shard_map/ppermute | solution.py:28
  22.2 6.2 %collective-permute-start.2 = (bf16[512,256]{1,0:T(8,128)(2,1)S(1)}, bf16[512,256]{1,0:T(8,128)(2,1)S(1)}, u32[]{:S(2)}, u32[]{:S(2)}) collective-permute-start(bf16[512,256]{1,0:T(8,128)(2,1)S(1)} %collective-permute-done.refs_4_), channel_id=1, source_target_pairs={{1,0},{0,1},{3,2},{2,3},{5,4},{4,5},{7,6},{6,7},{9,8},{8,9},{11,10... | collective-permute-start | bytes 786440 | tf_op jit(solution)/shard_map/ppermute | solution.py:28
  25.3 8.0 %collective-permute-start.9 = (bf16[512,256]{1,0:T(8,128)(2,1)S(1)}, bf16[512,256]{1,0:T(8,128)(2,1)S(1)}, u32[]{:S(2)}, u32[]{:S(2)}) collective-permute-start(bf16[512,256]{1,0:T(8,128)(2,1)S(1)} %collective-permute-done.8.refs_6_), channel_id=1, source_target_pairs={{2,0},{3,1},{0,2},{1,3},{6,4},{7,5},{4,6},{5,7},{10,8},{11,9},{8,1... | collective-permute-start | bytes 786440 | tf_op jit(solution)/shard_map/ppermute | solution.py:28
  26.8 6.6 %collective-permute-start.3 = (bf16[512,256]{1,0:T(8,128)(2,1)S(1)}, bf16[512,256]{1,0:T(8,128)(2,1)}, u32[]{:S(2)}, u32[]{:S(2)}) collective-permute-start(bf16[512,256]{1,0:T(8,128)(2,1)S(1)} %collective-permute-done.1.refs_5_), channel_id=1, source_target_pairs={{1,0},{0,1},{3,2},{2,3},{5,4},{4,5},{7,6},{6,7},{9,8},{8,9},{11,10... | collective-permute-start | bytes 786440 | tf_op jit(solution)/shard_map/ppermute | solution.py:28
  26.8 10.4 %collective-permute-start.6 = (bf16[512,256]{1,0:T(8,128)(2,1)S(1)}, bf16[512,256]{1,0:T(8,128)(2,1)S(1)}, u32[]{:S(2)}, u32[]{:S(2)}) collective-permute-start(bf16[512,256]{1,0:T(8,128)(2,1)S(1)} %collective-permute-done.4.refs_6_), channel_id=1, source_target_pairs={{1,0},{0,1},{3,2},{2,3},{5,4},{4,5},{7,6},{6,7},{9,8},{8,9},{11,10... | collective-permute-start | bytes 786440 | tf_op jit(solution)/shard_map/ppermute | solution.py:28
  28.4 8.8 %collective-permute-start.7 = (bf16[512,256]{1,0:T(8,128)(2,1)S(1)}, bf16[512,256]{1,0:T(8,128)(2,1)S(1)}, u32[]{:S(2)}, u32[]{:S(2)}) collective-permute-start(bf16[512,256]{1,0:T(8,128)(2,1)S(1)} %collective-permute-done.5.refs_7_), channel_id=1, source_target_pairs={{1,0},{0,1},{3,2},{2,3},{5,4},{4,5},{7,6},{6,7},{9,8},{8,9},{11,10... | collective-permute-start | bytes 786440 | tf_op jit(solution)/shard_map/ppermute | solution.py:28
  28.4 11.1 %collective-permute-start.10 = (bf16[512,256]{1,0:T(8,128)(2,1)S(1)}, bf16[512,256]{1,0:T(8,128)(2,1)S(1)}, u32[]{:S(2)}, u32[]{:S(2)}) collective-permute-start(bf16[512,256]{1,0:T(8,128)(2,1)S(1)} %collective-permute-done.8.refs_6_), channel_id=1, source_target_pairs={{1,0},{0,1},{3,2},{2,3},{5,4},{4,5},{7,6},{6,7},{9,8},{8,9},{11,10... | collective-permute-start | bytes 786440 | tf_op jit(solution)/shard_map/ppermute | solution.py:28
  33.3 6.2 %collective-permute-start.11 = (bf16[512,256]{1,0:T(8,128)(2,1)S(1)}, bf16[512,256]{1,0:T(8,128)(2,1)S(1)}, u32[]{:S(2)}, u32[]{:S(2)}) collective-permute-start(bf16[512,256]{1,0:T(8,128)(2,1)S(1)} %collective-permute-done.9.refs_7_), channel_id=1, source_target_pairs={{1,0},{0,1},{3,2},{2,3},{5,4},{4,5},{7,6},{6,7},{9,8},{8,9},{11,10... | collective-permute-start | bytes 786440 | tf_op jit(solution)/shard_map/ppermute | solution.py:28
  33.4 0.7 %copy-start.2 = (f32[3,256]{1,0:T(4,128)S(1)}, f32[3,256]{1,0:T(4,128)}, u32[]{:S(2)}) copy-start(f32[3,256]{1,0:T(4,128)} %refs_3_.5) | copy-start | bytes 9220

commit v2 on v0

v2 whole, which is shorter than its diff:
```python
import functools
import math

import jax
import jax.numpy as jnp
from jax import lax
from jax.experimental import pallas as pl
from jax.experimental.pallas import tpu as pltpu
from jax.sharding import PartitionSpec as P


score_factor = 2.5
unusable = 32.0
usable_limit = 16.0
lanes = 128
row_block = 256
vmem = pl.BlockSpec(memory_space=pltpu.VMEM)
smem = pl.BlockSpec(memory_space=pltpu.SMEM)
grant = pltpu.CompilerParams(vmem_limit_bytes=24 * 2**20)


def from_behind(block, distance):
    n = lax.axis_size("sec")
    return lax.ppermute(block, "sec", [((i - distance) % n, i) for i in range(n)])


def from_partner(block, distance):
    n = lax.axis_size("tile")
    return lax.ppermute(block, "tile", [(i ^ distance, i) for i in range(n)])


def widen(column, channels):
    return jnp.concatenate([column] * (channels // lanes), axis=1)


def is_usable(tile_ref):
    mark = tile_ref[0:8, 0:lanes].astype(jnp.float32)[0:1, :]
    return jnp.where(mark <= usable_limit, 1.0, 0.0)


def matched(queries, key_refs, scale):
    step = scale * math.log2(math.e)
    scores = [
        lax.dot_general(
            queries, k[...], (((1,), (1,)), ((), ())), preferred_element_type=jnp.float32
        )
        for k in key_refs
    ]
    top = functools.reduce(jnp.maximum, [s.max(axis=1, keepdims=True) for s in scores]) * step
    total = 0.0
    weighted = 0.0
    for s, k in zip(scores, key_refs):
        weights = jnp.exp2(s * step - top)
        total = total + jnp.sum(weights, axis=1, keepdims=True)
        weighted = weighted + jnp.dot(
            weights.astype(jnp.bfloat16), k[...], preferred_element_type=jnp.float32
        )
    return weighted, total


def chosen_rows(columns, offset, section_ref, usable):
    behind = (section_ref[0] >= offset).astype(jnp.float32)
    bits = (columns >> (offset - 1)) & 1
    return bits.astype(jnp.float32) * (usable * behind)


def prepare(select_ref, columns_ref):
    rows = jnp.broadcast_to(select_ref[...].astype(jnp.float32), (lanes, select_ref.shape[1]))
    columns_ref[...] = rows.T.astype(jnp.int32)


def answer(scale, query_ref, *refs):
    *key_refs, out_ref = refs
    num_rows, channels = query_ref.shape
    keep = widen(is_usable(key_refs[0]), channels) > 0.5
    for row in range(0, num_rows, row_block):
        rows = slice(row, row + row_block)
        weighted, total = matched(query_ref[rows, :], key_refs, scale)
        out_ref[rows, :] = jnp.where(keep, weighted / total, unusable).astype(jnp.bfloat16)


def fold(offset, first, scale, section_ref, query_ref, columns_ref, gain_ref, *refs):
    if not first:
        numerator_ref, count_ref, *refs = refs
    *key_refs, out_ref, count_out_ref = refs
    num_rows, channels = query_ref.shape
    usable = is_usable(key_refs[0])
    gain = gain_ref[offset - 1 : offset, :]
    for row in range(0, num_rows, row_block):
        rows = slice(row, row + row_block)
        weighted, total = matched(query_ref[rows, :], key_refs, scale)
        count = chosen_rows(columns_ref[rows, :], offset, section_ref, usable)
        numerator = weighted * widen(count / total, channels) * gain
        if not first:
            numerator = numerator + numerator_ref[rows, :]
            count = count + count_ref[rows, :]
        out_ref[rows, :] = numerator
        count_out_ref[rows, :] = count


def finish(
    offset, section_ref, columns_ref, gain_ref, numerator_ref, count_ref, warped_ref, out_ref
):
    _, channels = warped_ref.shape
    usable = is_usable(warped_ref)
    gain = gain_ref[offset - 1 : offset, :]
    chosen = chosen_rows(columns_ref[...], offset, section_ref, usable)
    divisor = jnp.maximum(count_ref[...] + chosen, 1.0)
    numerator = numerator_ref[...] + (
        warped_ref[...].astype(jnp.float32) * widen(chosen, channels) * gain
    )
    out_ref[...] = (numerator / widen(divisor, channels)).astype(jnp.bfloat16)


def shards(features, select, validity, offset_gain):
    queries = features[0]
    num_rows, channels = queries.shape
    scale = score_factor / math.sqrt(channels)
    section = lax.axis_index("sec").astype(jnp.int32)[None]
    wide = jax.ShapeDtypeStruct((num_rows, channels), jnp.float32)
    tile = jax.ShapeDtypeStruct((num_rows, channels), jnp.bfloat16)
    narrow = jax.ShapeDtypeStruct((num_rows, lanes), jnp.float32)
    keys = num_rows * lax.axis_size("tile")
    heavy = pl.CostEstimate(
        flops=4 * num_rows * keys * channels,
        transcendentals=num_rows * keys,
        bytes_accessed=2 * keys * channels,
    )

    def call(body, out, args, cost=None, scalars=0):
        return pl.pallas_call(
            body,
            out_shape=out,
            in_specs=[smem] * scalars + [vmem] * (len(args) - scalars),
            out_specs=jax.tree.map(lambda _: vmem, out),
            cost_estimate=cost,
            compiler_params=grant,
        )(*args)

    def all_tiles(t):
        tiles = [t]
        distance = lax.axis_size("tile") // 2
        while distance:
            for held in tuple(tiles):
                tiles.append(from_partner(held, distance))
            distance //= 2
        return tiles

    columns_shape = jax.ShapeDtypeStruct((num_rows, lanes), jnp.int32)
    columns = call(prepare, columns_shape, (select,))
    sent = jnp.where(validity[0] != 0, queries, jnp.bfloat16(unusable))
    second = from_behind(sent, 2)
    first = from_behind(sent, 1)
    ahead = from_behind(queries, -1)
    second_tiles = all_tiles(second)
    first_tiles = all_tiles(first)
    answered = call(functools.partial(answer, scale), tile, (ahead, *second_tiles), heavy)
    third = from_behind(answered, 1)
    common = (section, queries, columns, offset_gain)
    state = call(
        functools.partial(fold, 2, True, scale), (wide, narrow), (*common, *second_tiles), heavy, 1
    )
    state = call(
        functools.partial(fold, 1, False, scale),
        (wide, narrow),
        (*common, *state, *first_tiles),
        heavy,
        1,
    )
    out = call(
        functools.partial(finish, 3),
        tile,
        (section, columns, offset_gain, *state, third),
        scalars=1,
    )
    return out[None]


def solution(mesh):
    in_specs = (P("sec", "tile", None), P("sec", "tile"), P("sec"), P())
    out_specs = P("sec", "tile", None)

    def step(*arrays):
        return shards(*arrays)

    step = jax.shard_map(step, mesh=mesh, in_specs=in_specs, out_specs=out_specs, check_vma=False)
    return step
```

time: 85.1 us -> 41.8 us (0.49)
  starting transfers between devices: 28.1 us -> 8.28 us
  between operations: 15.8 us -> 0.75 us
  matrix products: 9.81 us -> 0 us
  Pallas kernels: 0 us -> 7.81 us
  waiting for transfers between devices: 24.9 us -> 22.4 us
  other arithmetic: 3.2 us -> 1.04 us
  local copies, waits for them, and re-layouts: 2.96 us -> 1.23 us
    ppermute x6 -> x10, starting transfers between devices: 28 us -> 8.28 us  [the longest x4 4.66 us: from_behind(): lax.ppermute(block, 'sec', [((i - distance) % n, i) for i in range(n)])]
    all_gather x3 -> x0, waiting for transfers between devices: 12.4 us -> none  [shards(): lax.all_gather(received, 'tile', axis=1, tiled=True)]
    ppermute x6 -> x10, waiting for transfers between devices: 12.4 us -> 22.4 us  [the longest x4 17.3 us: from_behind(): lax.ppermute(block, 'sec', [((i - distance) % n, i) for i in range(n)])]
    dot_general x6 -> x0, matrix products: 9.81 us -> none  [the longest x3 6.5 us: fold_step(): jnp.dot(queries, key_rows.T, preferred_element_type=jnp.float32)]
    pallas_call x0 -> x5, Pallas kernels: none -> 7.81 us  [call(): pl.pallas_call(body, out_shape=out, in_specs=[smem] * scalars + [vmem] *...]
    reduce_sum x3 -> x0, other arithmetic: 2.47 us -> none  [fold_step(): running_sum = jnp.sum(weights, axis=1)]
    select_n x0 -> x1, other arithmetic: none -> 1.04 us  [shards(): sent = jnp.where(validity[0] != 0, queries, jnp.bfloat16(unusable))]
    unnamed x14 -> x6, local copies, waits for them, and re-layouts: 2.16 us -> 1.23 us
  transfers between devices with their start and end apart: 9 -> 10, of which waited for: 5 -> 5; matrix products, arithmetic and copies ran while one was open for 11% -> 0% of each run, Pallas kernels for 0% -> 17%
where the time goes in v2:
time: 41.8 us; the launch traced here: 41.5 us
  waiting for transfers between devices  22.4 us (54%)
  starting transfers between devices  8.28 us (20%)
  Pallas kernels  7.81 us (19%)
  local copies, waits for them, and re-layouts  1.23 us (3%)
  other arithmetic  1.04 us (2%)
  between operations  0.75 us (2%)
    ppermute x4, waiting for transfers between devices, from_behind(): lax.ppermute(block, 'sec', [((i - distance) % n, i) for i in range(n)])  17.3 us
    pallas_call x5, Pallas kernels, call(): pl.pallas_call(body, out_shape=out, in_specs=[smem] * scalars + [vmem] *...  7.81 us
    ppermute x6, waiting for transfers between devices, from_partner(): return lax.ppermute(block, 'tile', [(i ^ distance, i) for i in range(n)])  5.15 us
    ppermute x4, starting transfers between devices, from_behind(): lax.ppermute(block, 'sec', [((i - distance) % n, i) for i in range(n)])  4.66 us
    ppermute x6, starting transfers between devices, from_partner(): return lax.ppermute(block, 'tile', [(i ^ distance, i) for i in range(n)])  3.62 us
    unnamed x6, local copies, waits for them, and re-layouts  1.23 us
    select_n x1, other arithmetic, shards(): sent = jnp.where(validity[0] != 0, queries, jnp.bfloat16(unusable))  1.04 us
  transfers between devices with their start and end apart: 10, of which 5 were waited for; matrix products, arithmetic and copies ran while one was open for 0% of the time, Pallas kernels for 17%

profile of v2, /device:TPU:0, one launch (start us, length us, event | category | flops | bytes accessed | tf_op | source)
XLA Modules:
  0.0 41.5 jit_solution(8053381299211209414)
XLA Ops:
  0.7 1.0 %broadcast_select_fusion = bf16[512,256]{1,0:T(8,128)(2,1)S(1)} fusion(pred[]{:T(512)} %bitcast.2, bf16[1,512,256]{2,1,0:T(8,128)(2,1)} %param.4), kind=kLoop, calls=%fused_computation | loop fusion | flops 131072 | bytes 524289 | tf_op jit(solution)/shard_map/jit(_where)/select_n | solution.py:151
  1.7 3.1 %collective-permute-start = (bf16[512,256]{1,0:T(8,128)(2,1)S(1)}, bf16[512,256]{1,0:T(8,128)(2,1)S(1)}, u32[]{:S(2)}, u32[]{:S(2)}) collective-permute-start(bf16[512,256]{1,0:T(8,128)(2,1)S(1)} %broadcast_select_fusion), channel_id=1, source_target_pairs={{24,0},{28,4},{0,8},{4,12},{8,16},{12,20},{16,24},{20,28},{25,1},{... | collective-permute-start | bytes 786440 | tf_op jit(solution)/shard_map/ppermute | solution.py:24
  4.8 1.5 %collective-permute-start.4 = (bf16[512,256]{1,0:T(8,128)(2,1)S(1)}, bf16[512,256]{1,0:T(8,128)(2,1)S(1)}, u32[]{:S(2)}, u32[]{:S(2)}) collective-permute-start(bf16[512,256]{1,0:T(8,128)(2,1)S(1)} %broadcast_select_fusion), channel_id=1, source_target_pairs={{28,0},{0,4},{4,8},{8,12},{12,16},{16,20},{20,24},{24,28},{29,1},{... | collective-permute-start | bytes 786440 | tf_op jit(solution)/shard_map/ppermute | solution.py:24
  6.3 6.8 %collective-permute-done.refs_0_ = bf16[512,256]{1,0:T(8,128)(2,1)S(1)} collective-permute-done((bf16[512,256]{1,0:T(8,128)(2,1)S(1)}, bf16[512,256]{1,0:T(8,128)(2,1)S(1)}, u32[]{:S(2)}, u32[]{:S(2)}) %collective-permute-start) | collective-permute-done | bytes 262176 | tf_op jit(solution)/shard_map/ppermute | solution.py:24
  13.1 1.5 %collective-permute-start.1 = (bf16[512,256]{1,0:T(8,128)(2,1)S(1)}, bf16[512,256]{1,0:T(8,128)(2,1)S(1)}, u32[]{:S(2)}, u32[]{:S(2)}) collective-permute-start(bf16[512,256]{1,0:T(8,128)(2,1)S(1)} %collective-permute-done.refs_0_), channel_id=1, source_target_pairs={{2,0},{3,1},{0,2},{1,3},{6,4},{7,5},{4,6},{5,7},{10,8},{11,9},{8,1... | collective-permute-start | bytes 786440 | tf_op jit(solution)/shard_map/ppermute | solution.py:29
  14.7 5.0 %collective-permute-done.4.refs_2_ = bf16[512,256]{1,0:T(8,128)(2,1)S(1)} collective-permute-done((bf16[512,256]{1,0:T(8,128)(2,1)S(1)}, bf16[512,256]{1,0:T(8,128)(2,1)S(1)}, u32[]{:S(2)}, u32[]{:S(2)}) %collective-permute-start.4) | collective-permute-done | bytes 262176 | tf_op jit(solution)/shard_map/ppermute | solution.py:24
  19.7 1.5 %collective-permute-start.5 = (bf16[512,256]{1,0:T(8,128)(2,1)S(1)}, bf16[512,256]{1,0:T(8,128)(2,1)S(1)}, u32[]{:S(2)}, u32[]{:S(2)}) collective-permute-start(bf16[512,256]{1,0:T(8,128)(2,1)S(1)} %collective-permute-done.4.refs_2_), channel_id=1, source_target_pairs={{2,0},{3,1},{0,2},{1,3},{6,4},{7,5},{4,6},{5,7},{10,8},{11,9},{8,1... | collective-permute-start | bytes 786440 | tf_op jit(solution)/shard_map/ppermute | solution.py:29
  21.2 0.0 collective-permute-done.1.refs_1_
  21.2 0.5 %collective-permute-start.3 = (bf16[512,256]{1,0:T(8,128)(2,1)S(1)}, bf16[512,256]{1,0:T(8,128)(2,1)S(1)}, u32[]{:S(2)}, u32[]{:S(2)}) collective-permute-start(bf16[512,256]{1,0:T(8,128)(2,1)S(1)} %collective-permute-done.1.refs_1_), channel_id=1, source_target_pairs={{1,0},{0,1},{3,2},{2,3},{5,4},{4,5},{7,6},{6,7},{9,8},{8,9},{11,10... | collective-permute-start | bytes 786440 | tf_op jit(solution)/shard_map/ppermute | solution.py:29
  21.7 0.1 collective-permute-start.6
  21.8 5.1 %collective-permute-done.5.refs_3_ = bf16[512,256]{1,0:T(8,128)(2,1)S(1)} collective-permute-done((bf16[512,256]{1,0:T(8,128)(2,1)S(1)}, bf16[512,256]{1,0:T(8,128)(2,1)S(1)}, u32[]{:S(2)}, u32[]{:S(2)}) %collective-permute-start.5) | collective-permute-done | bytes 262176 | tf_op jit(solution)/shard_map/ppermute | solution.py:29
  26.9 0.0 collective-permute-start.7
  26.9 1.2 %collective-permute-done.8.query_ref = bf16[512,256]{1,0:T(8,128)(2,1)S(1)} collective-permute-done((bf16[512,256]{1,0:T(8,128)(2,1)S(1)}, bf16[512,256]{1,0:T(8,128)(2,1)S(1)}, u32[]{:S(2)}, u32[]{:S(2)}) %collective-permute-start.8) | collective-permute-done | bytes 262176 | tf_op jit(solution)/shard_map/ppermute | solution.py:24
  28.2 2.2 %shard_map.49 = bf16[512,256]{1,0:T(8,128)(2,1)S(1)} custom-call(bf16[512,256]{1,0:T(8,128)(2,1)S(1)} %collective-permute-done.8.query_ref, bf16[512,256]{1,0:T(8,128)(2,1)S(1)} %collective-permute-done.refs_0_, bf16[512,256]{1,0:T(8,128)(2,1)S(1)} %collective-permute-done.1.refs_1_, bf16[512,256]{1,0:T(8,128)(2,1)S(1)} %collective-permute-done.2.refs_2_, ...), custom_call_target="tpu_custom_call" | custom-call | flops 1073741824 | bytes 1048576 | tf_op jit(solution)/shard_map/pallas_call | solution.py:131
  30.4 0.1 collective-permute-start.9
  30.5 0.0 copy-start.2
  30.5 0.7 %copy-done.2 = s32[1,512]{1,0:T(1,128)S(1)} copy-done((s32[1,512]{1,0:T(1,128)S(1)}, s32[1,512]{1,0:T(1,128)}, u32[]{:S(2)}) %copy-start.2) | copy-done | bytes 2072
  31.2 0.1 shard_map.46.columns_ref
  31.3 0.5 %copy-done.1 = f32[3,256]{1,0:T(4,128)S(1)} copy-done((f32[3,256]{1,0:T(4,128)S(1)}, f32[3,256]{1,0:T(4,128)}, u32[]{:S(2)}) %copy-start.1) | copy-done | bytes 3096
  31.9 2.3 %shard_map.47 = (f32[512,256]{1,0:T(8,128)S(1)}, f32[512,128]{1,0:T(8,128)S(1)}) custom-call(s32[1]{0:T(128)} %bitcast.section_ref, bf16[512,256]{1,0:T(8,128)(2,1)S(1)} %bitcast.6, s32[512,128]{1,0:T(8,128)S(1)} %shard_map.46.columns_ref, f32[3,256]{1,0:T(4,128)S(1)} %copy-done.1, bf16[512,256]{1,0:T(8,128)(2,1)S(1)} %collective-permute-done.refs_0_, ...), custom_call_target="tpu_custom_call" | custom-call | flops 1073741824 | bytes 1048576 | tf_op jit(solution)/shard_map/pallas_call | solution.py:131
  34.1 0.0 collective-permute-done.6.refs_4_
  34.2 2.3 %shard_map.48 = (f32[512,256]{1,0:T(8,128)S(1)}, f32[512,128]{1,0:T(8,128)S(1)}) custom-call(s32[1]{0:T(128)} %bitcast.section_ref, bf16[512,256]{1,0:T(8,128)(2,1)S(1)} %bitcast.7, s32[512,128]{1,0:T(8,128)S(1)} %shard_map.46.columns_ref, f32[3,256]{1,0:T(4,128)S(1)} %copy-done.1, f32[512,256]{1,0:T(8,128)S(1)} %get-tuple-element.9.refs_0_, ...), custom_call_target="tpu_custom_call" | custom-call | flops 1073741824 | bytes 1048576 | tf_op jit(solution)/shard_map/pallas_call | solution.py:131
  36.5 4.2 %collective-permute-done.9.warped_ref = bf16[512,256]{1,0:T(8,128)(2,1)S(1)} collective-permute-done((bf16[512,256]{1,0:T(8,128)(2,1)S(1)}, bf16[512,256]{1,0:T(8,128)(2,1)S(1)}, u32[]{:S(2)}, u32[]{:S(2)}) %collective-permute-start.9) | collective-permute-done | bytes 262176 | tf_op jit(solution)/shard_map/ppermute | solution.py:24
  40.7 0.9 %shard_map.50 = bf16[512,256]{1,0:T(8,128)(2,1)} custom-call(s32[1]{0:T(128)} %bitcast.section_ref, s32[512,128]{1,0:T(8,128)S(1)} %shard_map.46.columns_ref, f32[3,256]{1,0:T(4,128)S(1)} %copy-done.1, f32[512,256]{1,0:T(8,128)S(1)} %get-tuple-element.11.numerator_ref, f32[512,128]{1,0:T(8,128)S(1)} %get-tuple-element.12.count_ref, ...), custom_call_target="tpu_custom_call" | custom-call | tf_op jit(solution)/shard_map/pallas_call | solution.py:131
  (8 shorter events, 0.0 us)
Async XLA Ops:
  0.7 20.6 %copy-start = (bf16[1,512,256]{2,1,0:T(8,128)(2,1)S(1)}, bf16[1,512,256]{2,1,0:T(8,128)(2,1)}, u32[]{:S(2)}) copy-start(bf16[1,512,256]{2,1,0:T(8,128)(2,1)} %param.4) | copy-start | bytes 786436
  1.7 11.4 %collective-permute-start = (bf16[512,256]{1,0:T(8,128)(2,1)S(1)}, bf16[512,256]{1,0:T(8,128)(2,1)S(1)}, u32[]{:S(2)}, u32[]{:S(2)}) collective-permute-start(bf16[512,256]{1,0:T(8,128)(2,1)S(1)} %broadcast_select_fusion), channel_id=1, source_target_pairs={{24,0},{28,4},{0,8},{4,12},{8,16},{12,20},{16,24},{20,28},{25,1},{... | collective-permute-start | bytes 786440 | tf_op jit(solution)/shard_map/ppermute | solution.py:24
  4.8 14.9 %collective-permute-start.4 = (bf16[512,256]{1,0:T(8,128)(2,1)S(1)}, bf16[512,256]{1,0:T(8,128)(2,1)S(1)}, u32[]{:S(2)}, u32[]{:S(2)}) collective-permute-start(bf16[512,256]{1,0:T(8,128)(2,1)S(1)} %broadcast_select_fusion), channel_id=1, source_target_pairs={{28,0},{0,4},{4,8},{8,12},{12,16},{16,20},{20,24},{24,28},{29,1},{... | collective-permute-start | bytes 786440 | tf_op jit(solution)/shard_map/ppermute | solution.py:24
  13.1 8.1 %collective-permute-start.1 = (bf16[512,256]{1,0:T(8,128)(2,1)S(1)}, bf16[512,256]{1,0:T(8,128)(2,1)S(1)}, u32[]{:S(2)}, u32[]{:S(2)}) collective-permute-start(bf16[512,256]{1,0:T(8,128)(2,1)S(1)} %collective-permute-done.refs_0_), channel_id=1, source_target_pairs={{2,0},{3,1},{0,2},{1,3},{6,4},{7,5},{4,6},{5,7},{10,8},{11,9},{8,1... | collective-permute-start | bytes 786440 | tf_op jit(solution)/shard_map/ppermute | solution.py:29
  19.7 7.3 %collective-permute-start.5 = (bf16[512,256]{1,0:T(8,128)(2,1)S(1)}, bf16[512,256]{1,0:T(8,128)(2,1)S(1)}, u32[]{:S(2)}, u32[]{:S(2)}) collective-permute-start(bf16[512,256]{1,0:T(8,128)(2,1)S(1)} %collective-permute-done.4.refs_2_), channel_id=1, source_target_pairs={{2,0},{3,1},{0,2},{1,3},{6,4},{7,5},{4,6},{5,7},{10,8},{11,9},{8,1... | collective-permute-start | bytes 786440 | tf_op jit(solution)/shard_map/ppermute | solution.py:29
  21.2 7.0 %collective-permute-start.8 = (bf16[512,256]{1,0:T(8,128)(2,1)S(1)}, bf16[512,256]{1,0:T(8,128)(2,1)S(1)}, u32[]{:S(2)}, u32[]{:S(2)}) collective-permute-start(bf16[512,256]{1,0:T(8,128)(2,1)S(1)} %bitcast.5), channel_id=1, source_target_pairs={{4,0},{8,4},{12,8},{16,12},{20,16},{24,20},{28,24},{0,28},{5,1},{9... | collective-permute-start | bytes 786440 | tf_op jit(solution)/shard_map/ppermute | solution.py:24
  21.2 7.0 %collective-permute-start.2 = (bf16[512,256]{1,0:T(8,128)(2,1)S(1)}, bf16[512,256]{1,0:T(8,128)(2,1)S(1)}, u32[]{:S(2)}, u32[]{:S(2)}) collective-permute-start(bf16[512,256]{1,0:T(8,128)(2,1)S(1)} %collective-permute-done.refs_0_), channel_id=1, source_target_pairs={{1,0},{0,1},{3,2},{2,3},{5,4},{4,5},{7,6},{6,7},{9,8},{8,9},{11,10... | collective-permute-start | bytes 786440 | tf_op jit(solution)/shard_map/ppermute | solution.py:29
  21.2 7.0 %collective-permute-start.3 = (bf16[512,256]{1,0:T(8,128)(2,1)S(1)}, bf16[512,256]{1,0:T(8,128)(2,1)S(1)}, u32[]{:S(2)}, u32[]{:S(2)}) collective-permute-start(bf16[512,256]{1,0:T(8,128)(2,1)S(1)} %collective-permute-done.1.refs_1_), channel_id=1, source_target_pairs={{1,0},{0,1},{3,2},{2,3},{5,4},{4,5},{7,6},{6,7},{9,8},{8,9},{11,10... | collective-permute-start | bytes 786440 | tf_op jit(solution)/shard_map/ppermute | solution.py:29
  21.7 12.4 %collective-permute-start.6 = (bf16[512,256]{1,0:T(8,128)(2,1)S(1)}, bf16[512,256]{1,0:T(8,128)(2,1)S(1)}, u32[]{:S(2)}, u32[]{:S(2)}) collective-permute-start(bf16[512,256]{1,0:T(8,128)(2,1)S(1)} %collective-permute-done.4.refs_2_), channel_id=1, source_target_pairs={{1,0},{0,1},{3,2},{2,3},{5,4},{4,5},{7,6},{6,7},{9,8},{8,9},{11,10... | collective-permute-start | bytes 786440 | tf_op jit(solution)/shard_map/ppermute | solution.py:29
  26.9 7.2 %collective-permute-start.7 = (bf16[512,256]{1,0:T(8,128)(2,1)S(1)}, bf16[512,256]{1,0:T(8,128)(2,1)S(1)}, u32[]{:S(2)}, u32[]{:S(2)}) collective-permute-start(bf16[512,256]{1,0:T(8,128)(2,1)S(1)} %collective-permute-done.5.refs_3_), channel_id=1, source_target_pairs={{1,0},{0,1},{3,2},{2,3},{5,4},{4,5},{7,6},{6,7},{9,8},{8,9},{11,10... | collective-permute-start | bytes 786440 | tf_op jit(solution)/shard_map/ppermute | solution.py:29
  30.4 10.2 %collective-permute-start.9 = (bf16[512,256]{1,0:T(8,128)(2,1)S(1)}, bf16[512,256]{1,0:T(8,128)(2,1)S(1)}, u32[]{:S(2)}, u32[]{:S(2)}) collective-permute-start(bf16[512,256]{1,0:T(8,128)(2,1)S(1)} %shard_map.49), channel_id=1, source_target_pairs={{28,0},{0,4},{4,8},{8,12},{12,16},{16,20},{20,24},{24,28},{29,1},{... | collective-permute-start | bytes 786440 | tf_op jit(solution)/shard_map/ppermute | solution.py:24
  30.5 0.7 %copy-start.2 = (s32[1,512]{1,0:T(1,128)S(1)}, s32[1,512]{1,0:T(1,128)}, u32[]{:S(2)}) copy-start(s32[1,512]{1,0:T(1,128)} %select_ref.1) | copy-start | bytes 6148
  31.2 0.7 %copy-start.1 = (f32[3,256]{1,0:T(4,128)S(1)}, f32[3,256]{1,0:T(4,128)}, u32[]{:S(2)}) copy-start(f32[3,256]{1,0:T(4,128)} %gain_ref.5) | copy-start | bytes 9220

commit v3 on v2

--- a/solution.py
+++ b/solution.py
@@ -13,6 +13,7 @@
 unusable = 32.0
 usable_limit = 16.0
 lanes = 128
+sublanes = 8
 row_block = 256
 vmem = pl.BlockSpec(memory_space=pltpu.VMEM)
 smem = pl.BlockSpec(memory_space=pltpu.SMEM)
@@ -22,6 +23,11 @@
 def from_behind(block, distance):
     n = lax.axis_size("sec")
     return lax.ppermute(block, "sec", [((i - distance) % n, i) for i in range(n)])
+
+
+def swapped(block, first):
+    pairs = [(i, i + 1) for i in range(first, lax.axis_size("sec") - 1, 2)]
+    return lax.ppermute(block, "sec", pairs + [(j, i) for i, j in pairs])
 
 
 def from_partner(block, distance):
@@ -64,38 +70,62 @@
     return bits.astype(jnp.float32) * (usable * behind)
 
 
-def prepare(select_ref, columns_ref):
+def prepare(select_ref, validity_ref, columns_ref, mark_ref):
+    mark_ref[...] = jnp.broadcast_to(validity_ref[...].astype(jnp.float32), mark_ref.shape)
     rows = jnp.broadcast_to(select_ref[...].astype(jnp.float32), (lanes, select_ref.shape[1]))
     columns_ref[...] = rows.T.astype(jnp.int32)
 
 
-def answer(scale, query_ref, *refs):
+def answer(scale, num_sections, section_ref, flag_ref, beside_ref, across_ref, *refs):
     *key_refs, out_ref = refs
-    num_rows, channels = query_ref.shape
-    keep = widen(is_usable(key_refs[0]), channels) > 0.5
-    for row in range(0, num_rows, row_block):
-        rows = slice(row, row + row_block)
-        weighted, total = matched(query_ref[rows, :], key_refs, scale)
-        out_ref[rows, :] = jnp.where(keep, weighted / total, unusable).astype(jnp.bfloat16)
-
-
-def fold(offset, first, scale, section_ref, query_ref, columns_ref, gain_ref, *refs):
+    num_rows, channels = out_ref.shape
+    section = section_ref[0]
+    needed = (section >= 2) & (section < num_sections - 1)
+
+    @pl.when(needed)
+    def _():
+        keep = jnp.broadcast_to(widen(flag_ref[0:1, :], channels), (row_block, channels)) > 0.5
+        for row in range(0, num_rows, row_block):
+            rows = slice(row, row + row_block)
+            queries = jnp.where(section % 2 == 1, across_ref[rows, :], beside_ref[rows, :])
+            weighted, total = matched(queries, key_refs, scale)
+            out_ref[rows, :] = jnp.where(keep, weighted / total, unusable).astype(jnp.bfloat16)
+
+    @pl.when(jnp.logical_not(needed))
+    def _():
+        out_ref[...] = jnp.full(out_ref.shape, unusable, jnp.bfloat16)
+
+
+def fold(offset, first, scale, section_ref, flag_ref, query_ref, columns_ref, gain_ref, *refs):
     if not first:
         numerator_ref, count_ref, *refs = refs
     *key_refs, out_ref, count_out_ref = refs
     num_rows, channels = query_ref.shape
-    usable = is_usable(key_refs[0])
+    usable = flag_ref[0:1, :]
     gain = gain_ref[offset - 1 : offset, :]
-    for row in range(0, num_rows, row_block):
-        rows = slice(row, row + row_block)
-        weighted, total = matched(query_ref[rows, :], key_refs, scale)
-        count = chosen_rows(columns_ref[rows, :], offset, section_ref, usable)
-        numerator = weighted * widen(count / total, channels) * gain
-        if not first:
-            numerator = numerator + numerator_ref[rows, :]
-            count = count + count_ref[rows, :]
-        out_ref[rows, :] = numerator
-        count_out_ref[rows, :] = count
+    needed = section_ref[0] >= offset
+
+    @pl.when(needed)
+    def _():
+        for row in range(0, num_rows, row_block):
+            rows = slice(row, row + row_block)
+            weighted, total = matched(query_ref[rows, :], key_refs, scale)
+            count = chosen_rows(columns_ref[rows, :], offset, section_ref, usable)
+            numerator = weighted * widen(count / total, channels) * gain
+            if not first:
+                numerator = numerator + numerator_ref[rows, :]
+                count = count + count_ref[rows, :]
+            out_ref[rows, :] = numerator
+            count_out_ref[rows, :] = count
+
+    @pl.when(jnp.logical_not(needed))
+    def _():
+        if first:
+            out_ref[...] = jnp.zeros_like(out_ref)
+            count_out_ref[...] = jnp.zeros_like(count_out_ref)
+        else:
+            out_ref[...] = numerator_ref[...]
+            count_out_ref[...] = count_ref[...]
 
 
 def finish(
@@ -147,23 +177,36 @@
         return tiles
 
     columns_shape = jax.ShapeDtypeStruct((num_rows, lanes), jnp.int32)
-    columns = call(prepare, columns_shape, (select,))
-    sent = jnp.where(validity[0] != 0, queries, jnp.bfloat16(unusable))
-    second = from_behind(sent, 2)
-    first = from_behind(sent, 1)
-    ahead = from_behind(queries, -1)
+    mark_shape = jax.ShapeDtypeStruct((sublanes, lanes), jnp.float32)
+    columns, mark = call(prepare, (columns_shape, mark_shape), (select, validity[:, None]))
+    second = from_behind(queries, 2)
+    beside = swapped(queries, 0)
+    across = swapped(queries, 1)
+    flag1 = from_behind(mark, 1)
+    flag2 = from_behind(mark, 2)
+    first = jnp.where(section[0] % 2 == 1, beside, across)
     second_tiles = all_tiles(second)
     first_tiles = all_tiles(first)
-    answered = call(functools.partial(answer, scale), tile, (ahead, *second_tiles), heavy)
+    answered = call(
+        functools.partial(answer, scale, lax.axis_size("sec")),
+        tile,
+        (section, flag2, beside, across, *second_tiles),
+        heavy,
+        1,
+    )
     third = from_behind(answered, 1)
-    common = (section, queries, columns, offset_gain)
+    common = (queries, columns, offset_gain)
     state = call(
-        functools.partial(fold, 2, True, scale), (wide, narrow), (*common, *second_tiles), heavy, 1
+        functools.partial(fold, 2, True, scale),
+        (wide, narrow),
+        (section, flag2, *common, *second_tiles),
+        heavy,
+        1,
     )
     state = call(
         functools.partial(fold, 1, False, scale),
         (wide, narrow),
-        (*common, *state, *first_tiles),
+        (section, flag1, *common, *state, *first_tiles),
         heavy,
         1,
     )

time: 41.8 us -> 40.7 us (0.974)
  the two profiles are of different devices: /device:TPU:0 before, /device:TPU:12 now
where the time goes in v3:
time: 40.7 us; the launch traced here: 40.5 us
  waiting for transfers between devices  19 us (47%)
  starting transfers between devices  12.9 us (32%)
  Pallas kernels  7.83 us (19%)
  between operations  0.75 us (2%)
    ppermute x2, waiting for transfers between devices, swapped(): return lax.ppermute(block, 'sec', pairs + [(j, i) for i, j in pairs])  9.48 us
    pallas_call x5, Pallas kernels, call(): pl.pallas_call(body, out_shape=out, in_specs=[smem] * scalars + [vmem] *...  7.83 us
    ppermute x4, starting transfers between devices, from_behind(): lax.ppermute(block, 'sec', [((i - distance) % n, i) for i in range(n)])  6.3 us
    ppermute x4, waiting for transfers between devices, from_behind(): lax.ppermute(block, 'sec', [((i - distance) % n, i) for i in range(n)])  6.05 us
    ppermute x2, starting transfers between devices, swapped(): return lax.ppermute(block, 'sec', pairs + [(j, i) for i, j in pairs])  5 us
    ppermute x6, waiting for transfers between devices, from_partner(): return lax.ppermute(block, 'tile', [(i ^ distance, i) for i in range(n)])  3.48 us
    ppermute x6, starting transfers between devices, from_partner(): return lax.ppermute(block, 'tile', [(i ^ distance, i) for i in range(n)])  1.59 us
  transfers between devices with their start and end apart: 12, of which 5 were waited for; matrix products, arithmetic and copies ran while one was open for 0% of the time, Pallas kernels for 17%

profile of v3, /device:TPU:12, one launch (start us, length us, event | category | flops | bytes accessed | tf_op | source)
XLA Modules:
  0.0 40.5 jit_solution(7833178233116929589)
XLA Ops:
  0.0 1.6 %collective-permute-start.2 = (bf16[512,256]{1,0:T(8,128)(2,1)}, bf16[512,256]{1,0:T(8,128)(2,1)S(1)}, u32[]{:S(2)}, u32[]{:S(2)}) collective-permute-start(bf16[512,256]{1,0:T(8,128)(2,1)} %bitcast.5), channel_id=1, source_target_pairs={{24,0},{28,4},{0,8},{4,12},{8,16},{12,20},{16,24},{20,28},{25,1},{... | collective-permute-start | bytes 786440 | tf_op jit(solution)/shard_map/ppermute | solution.py:25
  1.6 3.3 %collective-permute-start.7 = (bf16[512,256]{1,0:T(8,128)(2,1)}, bf16[512,256]{1,0:T(8,128)(2,1)S(1)}, u32[]{:S(2)}, u32[]{:S(2)}) collective-permute-start(bf16[512,256]{1,0:T(8,128)(2,1)} %bitcast.6), channel_id=1, source_target_pairs={{4,8},{12,16},{20,24},{8,4},{16,12},{24,20},{5,9},{13,17},{21,25},... | collective-permute-start | bytes 786440 | tf_op jit(solution)/shard_map/ppermute | solution.py:30
  4.9 1.7 %collective-permute-start.6 = (bf16[512,256]{1,0:T(8,128)(2,1)}, bf16[512,256]{1,0:T(8,128)(2,1)S(1)}, u32[]{:S(2)}, u32[]{:S(2)}) collective-permute-start(bf16[512,256]{1,0:T(8,128)(2,1)} %bitcast.7), channel_id=1, source_target_pairs={{0,4},{8,12},{16,20},{24,28},{4,0},{12,8},{20,16},{28,24},{1,5},{9... | collective-permute-start | bytes 786440 | tf_op jit(solution)/shard_map/ppermute | solution.py:30
  6.6 1.7 %collective-permute-done.2.refs_0_ = bf16[512,256]{1,0:T(8,128)(2,1)S(1)} collective-permute-done((bf16[512,256]{1,0:T(8,128)(2,1)}, bf16[512,256]{1,0:T(8,128)(2,1)S(1)}, u32[]{:S(2)}, u32[]{:S(2)}) %collective-permute-start.2) | collective-permute-done | bytes 262176 | tf_op jit(solution)/shard_map/ppermute | solution.py:25
  8.3 0.5 %collective-permute-start.3 = (bf16[512,256]{1,0:T(8,128)(2,1)S(1)}, bf16[512,256]{1,0:T(8,128)(2,1)S(1)}, u32[]{:S(2)}, u32[]{:S(2)}) collective-permute-start(bf16[512,256]{1,0:T(8,128)(2,1)S(1)} %collective-permute-done.2.refs_0_), channel_id=1, source_target_pairs={{2,0},{3,1},{0,2},{1,3},{6,4},{7,5},{4,6},{5,7},{10,8},{11,9},{8,1... | collective-permute-start | bytes 786440 | tf_op jit(solution)/shard_map/ppermute | solution.py:35
  8.8 6.1 %collective-permute-done.7.across_ref = bf16[512,256]{1,0:T(8,128)(2,1)S(1)} collective-permute-done((bf16[512,256]{1,0:T(8,128)(2,1)}, bf16[512,256]{1,0:T(8,128)(2,1)S(1)}, u32[]{:S(2)}, u32[]{:S(2)}) %collective-permute-start.7) | collective-permute-done | bytes 262176 | tf_op jit(solution)/shard_map/ppermute | solution.py:30
  14.9 3.3 %collective-permute-done.6.beside_ref = bf16[512,256]{1,0:T(8,128)(2,1)S(1)} collective-permute-done((bf16[512,256]{1,0:T(8,128)(2,1)}, bf16[512,256]{1,0:T(8,128)(2,1)S(1)}, u32[]{:S(2)}, u32[]{:S(2)}) %collective-permute-start.6) | collective-permute-done | bytes 262176 | tf_op jit(solution)/shard_map/ppermute | solution.py:30
  18.3 0.0 copy-start.1
  18.3 0.6 %collective-permute-start.8 = (bf16[512,256]{1,0:T(8,128)(2,1)S(1)}, bf16[512,256]{1,0:T(8,128)(2,1)S(1)}, u32[]{:S(2)}, u32[]{:S(2)}) collective-permute-start(bf16[512,256]{1,0:T(8,128)(2,1)S(1)} %broadcast_select_fusion.refs_2_), channel_id=1, source_target_pairs={{2,0},{3,1},{0,2},{1,3},{6,4},{7,5},{4,6},{5,7},{10,8},{11,9},{8,1... | collective-permute-start | bytes 786440 | tf_op jit(solution)/shard_map/ppermute | solution.py:35
  18.9 0.5 %collective-permute-start.5 = (bf16[512,256]{1,0:T(8,128)(2,1)S(1)}, bf16[512,256]{1,0:T(8,128)(2,1)S(1)}, u32[]{:S(2)}, u32[]{:S(2)}) collective-permute-start(bf16[512,256]{1,0:T(8,128)(2,1)S(1)} %collective-permute-done.3.refs_1_), channel_id=1, source_target_pairs={{1,0},{0,1},{3,2},{2,3},{5,4},{4,5},{7,6},{6,7},{9,8},{8,9},{11,10... | collective-permute-start | bytes 786440 | tf_op jit(solution)/shard_map/ppermute | solution.py:35
  20.0 0.2 shard_map.46
  20.2 1.6 %collective-permute-start.1 = (f32[8,128]{1,0:T(8,128)S(1)}, f32[8,128]{1,0:T(8,128)S(1)}, u32[]{:S(2)}, u32[]{:S(2)}) collective-permute-start(f32[8,128]{1,0:T(8,128)S(1)} %get-tuple-element.12), channel_id=1, source_target_pairs={{24,0},{28,4},{0,8},{4,12},{8,16},{12,20},{16,24},{20,28},{25,1},{... | collective-permute-start | bytes 12296 | tf_op jit(solution)/shard_map/ppermute | solution.py:25
  21.8 0.0 collective-permute-start.9
  21.8 3.5 %collective-permute-done.8.refs_3_ = bf16[512,256]{1,0:T(8,128)(2,1)S(1)} collective-permute-done((bf16[512,256]{1,0:T(8,128)(2,1)S(1)}, bf16[512,256]{1,0:T(8,128)(2,1)S(1)}, u32[]{:S(2)}, u32[]{:S(2)}) %collective-permute-start.8) | collective-permute-done | bytes 262176 | tf_op jit(solution)/shard_map/ppermute | solution.py:35
  25.3 0.0 collective-permute-start.10
  25.3 0.0 copy-start
  25.3 0.0 copy-start.2
  25.3 2.2 %shard_map.49 = bf16[512,256]{1,0:T(8,128)(2,1)S(1)} custom-call(s32[1]{0:T(128)} %bitcast.section_ref, f32[8,128]{1,0:T(8,128)S(1)} %collective-permute-done.1.flag_ref, bf16[512,256]{1,0:T(8,128)(2,1)S(1)} %collective-permute-done.6.beside_ref, bf16[512,256]{1,0:T(8,128)(2,1)S(1)} %collective-permute-done.7.across_ref, ...), custom_call_target="tpu_custom_call" | custom-call | flops 1073741824 | bytes 1048576 | tf_op jit(solution)/shard_map/pallas_call | solution.py:161
  27.6 1.7 %collective-permute-start.11 = (bf16[512,256]{1,0:T(8,128)(2,1)S(1)}, bf16[512,256]{1,0:T(8,128)(2,1)S(1)}, u32[]{:S(2)}, u32[]{:S(2)}) collective-permute-start(bf16[512,256]{1,0:T(8,128)(2,1)S(1)} %shard_map.49), channel_id=1, source_target_pairs={{28,0},{0,4},{4,8},{8,12},{12,16},{16,20},{20,24},{24,28},{29,1},{... | collective-permute-start | bytes 786440 | tf_op jit(solution)/shard_map/ppermute | solution.py:25
  29.3 1.4 %collective-permute-start = (f32[8,128]{1,0:T(8,128)S(1)}, f32[8,128]{1,0:T(8,128)S(1)}, u32[]{:S(2)}, u32[]{:S(2)}) collective-permute-start(f32[8,128]{1,0:T(8,128)S(1)} %get-tuple-element.12), channel_id=1, source_target_pairs={{28,0},{0,4},{4,8},{8,12},{12,16},{16,20},{20,24},{24,28},{29,1},{... | collective-permute-start | bytes 12296 | tf_op jit(solution)/shard_map/ppermute | solution.py:25
  30.6 2.3 %shard_map.47 = (f32[512,256]{1,0:T(8,128)S(1)}, f32[512,128]{1,0:T(8,128)S(1)}) custom-call(s32[1]{0:T(128)} %bitcast.section_ref, f32[8,128]{1,0:T(8,128)S(1)} %collective-permute-done.1.flag_ref, bf16[512,256]{1,0:T(8,128)(2,1)S(1)} %bitcast.8, s32[512,128]{1,0:T(8,128)S(1)} %get-tuple-element.11.columns_ref, f32[3,256]{1,0:T(4,128)S(1)} %copy-done, ...), custom_call_target="tpu_custom_call" | custom-call | flops 1073741824 | bytes 1048576 | tf_op jit(solution)/shard_map/pallas_call | solution.py:161
  32.9 4.4 %collective-permute-done.flag_ref = f32[8,128]{1,0:T(8,128)S(1)} collective-permute-done((f32[8,128]{1,0:T(8,128)S(1)}, f32[8,128]{1,0:T(8,128)S(1)}, u32[]{:S(2)}, u32[]{:S(2)}) %collective-permute-start) | collective-permute-done | bytes 4128 | tf_op jit(solution)/shard_map/ppermute | solution.py:25
  37.3 2.3 %shard_map.48 = (f32[512,256]{1,0:T(8,128)S(1)}, f32[512,128]{1,0:T(8,128)S(1)}) custom-call(s32[1]{0:T(128)} %bitcast.section_ref, f32[8,128]{1,0:T(8,128)S(1)} %collective-permute-done.flag_ref, bf16[512,256]{1,0:T(8,128)(2,1)S(1)} %bitcast.9, s32[512,128]{1,0:T(8,128)S(1)} %get-tuple-element.11.columns_ref, f32[3,256]{1,0:T(4,128)S(1)} %copy-done, ...), custom_call_target="tpu_custom_call" | custom-call | flops 1073741824 | bytes 1048576 | tf_op jit(solution)/shard_map/pallas_call | solution.py:161
  39.7 0.9 %shard_map.50 = bf16[512,256]{1,0:T(8,128)(2,1)} custom-call(s32[1]{0:T(128)} %bitcast.section_ref, s32[512,128]{1,0:T(8,128)S(1)} %get-tuple-element.11.columns_ref, f32[3,256]{1,0:T(4,128)S(1)} %copy-done, f32[512,256]{1,0:T(8,128)S(1)} %get-tuple-element.15.numerator_ref, f32[512,128]{1,0:T(8,128)S(1)} %get-tuple-element.16.count_ref, ...), custom_call_target="tpu_custom_call" | custom-call | tf_op jit(solution)/shard_map/pallas_call | solution.py:161
  (12 shorter events, 0.1 us)
Async XLA Ops:
  0.0 8.3 %collective-permute-start.2 = (bf16[512,256]{1,0:T(8,128)(2,1)}, bf16[512,256]{1,0:T(8,128)(2,1)S(1)}, u32[]{:S(2)}, u32[]{:S(2)}) collective-permute-start(bf16[512,256]{1,0:T(8,128)(2,1)} %bitcast.5), channel_id=1, source_target_pairs={{24,0},{28,4},{0,8},{4,12},{8,16},{12,20},{16,24},{20,28},{25,1},{... | collective-permute-start | bytes 786440 | tf_op jit(solution)/shard_map/ppermute | solution.py:25
  1.6 13.3 %collective-permute-start.7 = (bf16[512,256]{1,0:T(8,128)(2,1)}, bf16[512,256]{1,0:T(8,128)(2,1)S(1)}, u32[]{:S(2)}, u32[]{:S(2)}) collective-permute-start(bf16[512,256]{1,0:T(8,128)(2,1)} %bitcast.6), channel_id=1, source_target_pairs={{4,8},{12,16},{20,24},{8,4},{16,12},{24,20},{5,9},{13,17},{21,25},... | collective-permute-start | bytes 786440 | tf_op jit(solution)/shard_map/ppermute | solution.py:30
  4.9 13.4 %collective-permute-start.6 = (bf16[512,256]{1,0:T(8,128)(2,1)}, bf16[512,256]{1,0:T(8,128)(2,1)S(1)}, u32[]{:S(2)}, u32[]{:S(2)}) collective-permute-start(bf16[512,256]{1,0:T(8,128)(2,1)} %bitcast.7), channel_id=1, source_target_pairs={{0,4},{8,12},{16,20},{24,28},{4,0},{12,8},{20,16},{28,24},{1,5},{9... | collective-permute-start | bytes 786440 | tf_op jit(solution)/shard_map/ppermute | solution.py:30
  8.3 10.6 %collective-permute-start.3 = (bf16[512,256]{1,0:T(8,128)(2,1)S(1)}, bf16[512,256]{1,0:T(8,128)(2,1)S(1)}, u32[]{:S(2)}, u32[]{:S(2)}) collective-permute-start(bf16[512,256]{1,0:T(8,128)(2,1)S(1)} %collective-permute-done.2.refs_0_), channel_id=1, source_target_pairs={{2,0},{3,1},{0,2},{1,3},{6,4},{7,5},{4,6},{5,7},{10,8},{11,9},{8,1... | collective-permute-start | bytes 786440 | tf_op jit(solution)/shard_map/ppermute | solution.py:35
  18.3 1.8 %copy-start.1 = (s32[1,512]{1,0:T(1,128)S(1)}, s32[1,512]{1,0:T(1,128)}, u32[]{:S(2)}) copy-start(s32[1,512]{1,0:T(1,128)} %select_ref.1) | copy-start | bytes 6148
  18.3 7.0 %collective-permute-start.8 = (bf16[512,256]{1,0:T(8,128)(2,1)S(1)}, bf16[512,256]{1,0:T(8,128)(2,1)S(1)}, u32[]{:S(2)}, u32[]{:S(2)}) collective-permute-start(bf16[512,256]{1,0:T(8,128)(2,1)S(1)} %broadcast_select_fusion.refs_2_), channel_id=1, source_target_pairs={{2,0},{3,1},{0,2},{1,3},{6,4},{7,5},{4,6},{5,7},{10,8},{11,9},{8,1... | collective-permute-start | bytes 786440 | tf_op jit(solution)/shard_map/ppermute | solution.py:35
  18.9 6.5 %collective-permute-start.4 = (bf16[512,256]{1,0:T(8,128)(2,1)S(1)}, bf16[512,256]{1,0:T(8,128)(2,1)S(1)}, u32[]{:S(2)}, u32[]{:S(2)}) collective-permute-start(bf16[512,256]{1,0:T(8,128)(2,1)S(1)} %collective-permute-done.2.refs_0_), channel_id=1, source_target_pairs={{1,0},{0,1},{3,2},{2,3},{5,4},{4,5},{7,6},{6,7},{9,8},{8,9},{11,10... | collective-permute-start | bytes 786440 | tf_op jit(solution)/shard_map/ppermute | solution.py:35
  18.9 6.5 %collective-permute-start.5 = (bf16[512,256]{1,0:T(8,128)(2,1)S(1)}, bf16[512,256]{1,0:T(8,128)(2,1)S(1)}, u32[]{:S(2)}, u32[]{:S(2)}) collective-permute-start(bf16[512,256]{1,0:T(8,128)(2,1)S(1)} %collective-permute-done.3.refs_1_), channel_id=1, source_target_pairs={{1,0},{0,1},{3,2},{2,3},{5,4},{4,5},{7,6},{6,7},{9,8},{8,9},{11,10... | collective-permute-start | bytes 786440 | tf_op jit(solution)/shard_map/ppermute | solution.py:35
  20.2 5.1 %collective-permute-start.1 = (f32[8,128]{1,0:T(8,128)S(1)}, f32[8,128]{1,0:T(8,128)S(1)}, u32[]{:S(2)}, u32[]{:S(2)}) collective-permute-start(f32[8,128]{1,0:T(8,128)S(1)} %get-tuple-element.12), channel_id=1, source_target_pairs={{24,0},{28,4},{0,8},{4,12},{8,16},{12,20},{16,24},{20,28},{25,1},{... | collective-permute-start | bytes 12296 | tf_op jit(solution)/shard_map/ppermute | solution.py:25
  21.8 15.5 %collective-permute-start.9 = (bf16[512,256]{1,0:T(8,128)(2,1)S(1)}, bf16[512,256]{1,0:T(8,128)(2,1)S(1)}, u32[]{:S(2)}, u32[]{:S(2)}) collective-permute-start(bf16[512,256]{1,0:T(8,128)(2,1)S(1)} %broadcast_select_fusion.refs_2_), channel_id=1, source_target_pairs={{1,0},{0,1},{3,2},{2,3},{5,4},{4,5},{7,6},{6,7},{9,8},{8,9},{11,10... | collective-permute-start | bytes 786440 | tf_op jit(solution)/shard_map/ppermute | solution.py:35
  25.3 12.0 %collective-permute-start.10 = (bf16[512,256]{1,0:T(8,128)(2,1)S(1)}, bf16[512,256]{1,0:T(8,128)(2,1)S(1)}, u32[]{:S(2)}, u32[]{:S(2)}) collective-permute-start(bf16[512,256]{1,0:T(8,128)(2,1)S(1)} %collective-permute-done.8.refs_3_), channel_id=1, source_target_pairs={{1,0},{0,1},{3,2},{2,3},{5,4},{4,5},{7,6},{6,7},{9,8},{8,9},{11,10... | collective-permute-start | bytes 786440 | tf_op jit(solution)/shard_map/ppermute | solution.py:35
  25.3 5.3 %copy-start = (f32[3,256]{1,0:T(4,128)S(1)}, f32[3,256]{1,0:T(4,128)}, u32[]{:S(2)}) copy-start(f32[3,256]{1,0:T(4,128)} %gain_ref.5) | copy-start | bytes 9220
  25.3 5.3 %copy-start.2 = (bf16[1,512,256]{2,1,0:T(8,128)(2,1)S(1)}, bf16[1,512,256]{2,1,0:T(8,128)(2,1)}, u32[]{:S(2)}) copy-start(bf16[1,512,256]{2,1,0:T(8,128)(2,1)} %param.4) | copy-start | bytes 786436
  27.6 12.1 %collective-permute-start.11 = (bf16[512,256]{1,0:T(8,128)(2,1)S(1)}, bf16[512,256]{1,0:T(8,128)(2,1)S(1)}, u32[]{:S(2)}, u32[]{:S(2)}) collective-permute-start(bf16[512,256]{1,0:T(8,128)(2,1)S(1)} %shard_map.49), channel_id=1, source_target_pairs={{28,0},{0,4},{4,8},{8,12},{12,16},{16,20},{20,24},{24,28},{29,1},{... | collective-permute-start | bytes 786440 | tf_op jit(solution)/shard_map/ppermute | solution.py:25
  29.3 8.0 %collective-permute-start = (f32[8,128]{1,0:T(8,128)S(1)}, f32[8,128]{1,0:T(8,128)S(1)}, u32[]{:S(2)}, u32[]{:S(2)}) collective-permute-start(f32[8,128]{1,0:T(8,128)S(1)} %get-tuple-element.12), channel_id=1, source_target_pairs={{28,0},{0,4},{4,8},{8,12},{12,16},{16,20},{20,24},{24,28},{29,1},{... | collective-permute-start | bytes 12296 | tf_op jit(solution)/shard_map/ppermute | solution.py:25

commit v4 on v3

--- a/solution.py
+++ b/solution.py
@@ -70,8 +70,11 @@
     return bits.astype(jnp.float32) * (usable * behind)
 
 
-def prepare(select_ref, validity_ref, columns_ref, mark_ref):
+def note(validity_ref, mark_ref):
     mark_ref[...] = jnp.broadcast_to(validity_ref[...].astype(jnp.float32), mark_ref.shape)
+
+
+def prepare(select_ref, columns_ref):
     rows = jnp.broadcast_to(select_ref[...].astype(jnp.float32), (lanes, select_ref.shape[1]))
     columns_ref[...] = rows.T.astype(jnp.int32)
 
@@ -178,7 +181,8 @@
 
     columns_shape = jax.ShapeDtypeStruct((num_rows, lanes), jnp.int32)
     mark_shape = jax.ShapeDtypeStruct((sublanes, lanes), jnp.float32)
-    columns, mark = call(prepare, (columns_shape, mark_shape), (select, validity[:, None]))
+    columns = call(prepare, columns_shape, (select,))
+    mark = call(note, mark_shape, (validity[:, None],))
     second = from_behind(queries, 2)
     beside = swapped(queries, 0)
     across = swapped(queries, 1)
@@ -194,7 +198,9 @@
         heavy,
         1,
     )
-    third = from_behind(answered, 1)
+    n = lax.axis_size("sec")
+    routes = [(i, i + 1) for i in range(2, n - 1)] + [(0, 2), (1, 0), (n - 1, 1)]
+    third = lax.ppermute(answered, "sec", routes)
     common = (queries, columns, offset_gain)
     state = call(
         functools.partial(fold, 2, True, scale),

time: 40.7 us -> 40.7 us (level)
  the two profiles are of different devices: /device:TPU:12 before, /device:TPU:20 now
where the time goes in v4:
time: 40.7 us; the launch traced here: 40.5 us
  waiting for transfers between devices  20.3 us (50%)
  starting transfers between devices  11.5 us (28%)
  Pallas kernels  7.89 us (19%)
  between operations  0.77 us (2%)
    ppermute x2, waiting for transfers between devices, swapped(): return lax.ppermute(block, 'sec', pairs + [(j, i) for i, j in pairs])  9.48 us
    pallas_call x6, Pallas kernels, call(): pl.pallas_call(body, out_shape=out, in_specs=[smem] * scalars + [vmem] *...  7.89 us
    ppermute x3, waiting for transfers between devices, from_behind(): lax.ppermute(block, 'sec', [((i - distance) % n, i) for i in range(n)])  7.24 us
    ppermute x3, starting transfers between devices, from_behind(): lax.ppermute(block, 'sec', [((i - distance) % n, i) for i in range(n)])  5.75 us
    ppermute x2, starting transfers between devices, swapped(): return lax.ppermute(block, 'sec', pairs + [(j, i) for i, j in pairs])  3.65 us
    ppermute x6, waiting for transfers between devices, from_partner(): return lax.ppermute(block, 'tile', [(i ^ distance, i) for i in range(n)])  3.63 us
    ppermute x6, starting transfers between devices, from_partner(): return lax.ppermute(block, 'tile', [(i ^ distance, i) for i in range(n)])  1.59 us
  transfers between devices with their start and end apart: 12, of which 5 were waited for; matrix products, arithmetic and copies ran while one was open for 0% of the time, Pallas kernels for 17%

profile of v4, /device:TPU:20, one launch (start us, length us, event | category | flops | bytes accessed | tf_op | source)
XLA Modules:
  0.0 40.5 jit_solution(5941818158408277910)
XLA Ops:
  0.0 1.6 %collective-permute-start.2 = (bf16[512,256]{1,0:T(8,128)(2,1)}, bf16[512,256]{1,0:T(8,128)(2,1)S(1)}, u32[]{:S(2)}, u32[]{:S(2)}) collective-permute-start(bf16[512,256]{1,0:T(8,128)(2,1)} %bitcast.5), channel_id=1, source_target_pairs={{24,0},{28,4},{0,8},{4,12},{8,16},{12,20},{16,24},{20,28},{25,1},{... | collective-permute-start | bytes 786440 | tf_op jit(solution)/shard_map/ppermute | solution.py:25
  1.6 3.3 %collective-permute-start.7 = (bf16[512,256]{1,0:T(8,128)(2,1)}, bf16[512,256]{1,0:T(8,128)(2,1)S(1)}, u32[]{:S(2)}, u32[]{:S(2)}) collective-permute-start(bf16[512,256]{1,0:T(8,128)(2,1)} %bitcast.6), channel_id=1, source_target_pairs={{4,8},{12,16},{20,24},{8,4},{16,12},{24,20},{5,9},{13,17},{21,25},... | collective-permute-start | bytes 786440 | tf_op jit(solution)/shard_map/ppermute | solution.py:30
  4.9 0.4 collective-permute-start.6
  5.2 3.0 %collective-permute-done.2.refs_0_ = bf16[512,256]{1,0:T(8,128)(2,1)S(1)} collective-permute-done((bf16[512,256]{1,0:T(8,128)(2,1)}, bf16[512,256]{1,0:T(8,128)(2,1)S(1)}, u32[]{:S(2)}, u32[]{:S(2)}) %collective-permute-start.2) | collective-permute-done | bytes 262176 | tf_op jit(solution)/shard_map/ppermute | solution.py:25
  8.3 0.5 %collective-permute-start.3 = (bf16[512,256]{1,0:T(8,128)(2,1)S(1)}, bf16[512,256]{1,0:T(8,128)(2,1)S(1)}, u32[]{:S(2)}, u32[]{:S(2)}) collective-permute-start(bf16[512,256]{1,0:T(8,128)(2,1)S(1)} %collective-permute-done.2.refs_0_), channel_id=1, source_target_pairs={{2,0},{3,1},{0,2},{1,3},{6,4},{7,5},{4,6},{5,7},{10,8},{11,9},{8,1... | collective-permute-start | bytes 786440 | tf_op jit(solution)/shard_map/ppermute | solution.py:35
  8.8 6.1 %collective-permute-done.7.across_ref = bf16[512,256]{1,0:T(8,128)(2,1)S(1)} collective-permute-done((bf16[512,256]{1,0:T(8,128)(2,1)}, bf16[512,256]{1,0:T(8,128)(2,1)S(1)}, u32[]{:S(2)}, u32[]{:S(2)}) %collective-permute-start.7) | collective-permute-done | bytes 262176 | tf_op jit(solution)/shard_map/ppermute | solution.py:30
  14.9 3.3 %collective-permute-done.6.beside_ref = bf16[512,256]{1,0:T(8,128)(2,1)S(1)} collective-permute-done((bf16[512,256]{1,0:T(8,128)(2,1)}, bf16[512,256]{1,0:T(8,128)(2,1)S(1)}, u32[]{:S(2)}, u32[]{:S(2)}) %collective-permute-start.6) | collective-permute-done | bytes 262176 | tf_op jit(solution)/shard_map/ppermute | solution.py:30
  18.3 0.6 %collective-permute-start.8 = (bf16[512,256]{1,0:T(8,128)(2,1)S(1)}, bf16[512,256]{1,0:T(8,128)(2,1)S(1)}, u32[]{:S(2)}, u32[]{:S(2)}) collective-permute-start(bf16[512,256]{1,0:T(8,128)(2,1)S(1)} %broadcast_select_fusion.refs_2_), channel_id=1, source_target_pairs={{2,0},{3,1},{0,2},{1,3},{6,4},{7,5},{4,6},{5,7},{10,8},{11,9},{8,1... | collective-permute-start | bytes 786440 | tf_op jit(solution)/shard_map/ppermute | solution.py:35
  18.8 0.0 collective-permute-start.4
  18.9 0.5 %collective-permute-start.5 = (bf16[512,256]{1,0:T(8,128)(2,1)S(1)}, bf16[512,256]{1,0:T(8,128)(2,1)S(1)}, u32[]{:S(2)}, u32[]{:S(2)}) collective-permute-start(bf16[512,256]{1,0:T(8,128)(2,1)S(1)} %collective-permute-done.3.refs_1_), channel_id=1, source_target_pairs={{1,0},{0,1},{3,2},{2,3},{5,4},{4,5},{7,6},{6,7},{9,8},{8,9},{11,10... | collective-permute-start | bytes 786440 | tf_op jit(solution)/shard_map/ppermute | solution.py:35
  20.0 0.1 shard_map.47
  20.1 1.6 %collective-permute-start.1 = (f32[8,128]{1,0:T(8,128)S(1)}, f32[8,128]{1,0:T(8,128)S(1)}, u32[]{:S(2)}, u32[]{:S(2)}) collective-permute-start(f32[8,128]{1,0:T(8,128)S(1)} %shard_map.47), channel_id=1, source_target_pairs={{24,0},{28,4},{0,8},{4,12},{8,16},{12,20},{16,24},{20,28},{25,1},{... | collective-permute-start | bytes 12296 | tf_op jit(solution)/shard_map/ppermute | solution.py:25
  21.7 3.6 %collective-permute-done.8.refs_3_ = bf16[512,256]{1,0:T(8,128)(2,1)S(1)} collective-permute-done((bf16[512,256]{1,0:T(8,128)(2,1)S(1)}, bf16[512,256]{1,0:T(8,128)(2,1)S(1)}, u32[]{:S(2)}, u32[]{:S(2)}) %collective-permute-start.8) | collective-permute-done | bytes 262176 | tf_op jit(solution)/shard_map/ppermute | solution.py:35
  25.3 0.0 copy-start.1
  25.3 0.0 copy-start.2
  25.3 2.2 %shard_map.50 = bf16[512,256]{1,0:T(8,128)(2,1)S(1)} custom-call(s32[1]{0:T(128)} %bitcast.section_ref, f32[8,128]{1,0:T(8,128)S(1)} %collective-permute-done.1.flag_ref, bf16[512,256]{1,0:T(8,128)(2,1)S(1)} %collective-permute-done.6.beside_ref, bf16[512,256]{1,0:T(8,128)(2,1)S(1)} %collective-permute-done.7.across_ref, ...), custom_call_target="tpu_custom_call" | custom-call | flops 1073741824 | bytes 1048576 | tf_op jit(solution)/shard_map/pallas_call | solution.py:164
  27.5 0.0 copy-start
  27.6 0.5 %collective-permute-start.11 = (bf16[512,256]{1,0:T(8,128)(2,1)S(1)}, bf16[512,256]{1,0:T(8,128)(2,1)S(1)}, u32[]{:S(2)}, u32[]{:S(2)}) collective-permute-start(bf16[512,256]{1,0:T(8,128)(2,1)S(1)} %shard_map.50), channel_id=1, source_target_pairs={{8,12},{12,16},{16,20},{20,24},{24,28},{0,8},{4,0},{28,4},{9,13},{... | collective-permute-start | bytes 786440 | tf_op jit(solution)/shard_map/ppermute | solution.py:203
  28.0 2.6 %collective-permute-start = (f32[8,128]{1,0:T(8,128)S(1)}, f32[8,128]{1,0:T(8,128)S(1)}, u32[]{:S(2)}, u32[]{:S(2)}) collective-permute-start(f32[8,128]{1,0:T(8,128)S(1)} %shard_map.47), channel_id=1, source_target_pairs={{28,0},{0,4},{4,8},{8,12},{12,16},{16,20},{20,24},{24,28},{29,1},{... | collective-permute-start | bytes 12296 | tf_op jit(solution)/shard_map/ppermute | solution.py:25
  30.6 0.1 shard_map.46.columns_ref
  30.8 2.3 %shard_map.48 = (f32[512,256]{1,0:T(8,128)S(1)}, f32[512,128]{1,0:T(8,128)S(1)}) custom-call(s32[1]{0:T(128)} %bitcast.section_ref, f32[8,128]{1,0:T(8,128)S(1)} %collective-permute-done.1.flag_ref, bf16[512,256]{1,0:T(8,128)(2,1)S(1)} %bitcast.8, s32[512,128]{1,0:T(8,128)S(1)} %shard_map.46.columns_ref, f32[3,256]{1,0:T(4,128)S(1)} %copy-done, ...), custom_call_target="tpu_custom_call" | custom-call | flops 1073741824 | bytes 1048576 | tf_op jit(solution)/shard_map/pallas_call | solution.py:164
  33.1 4.2 %collective-permute-done.flag_ref = f32[8,128]{1,0:T(8,128)S(1)} collective-permute-done((f32[8,128]{1,0:T(8,128)S(1)}, f32[8,128]{1,0:T(8,128)S(1)}, u32[]{:S(2)}, u32[]{:S(2)}) %collective-permute-start) | collective-permute-done | bytes 4128 | tf_op jit(solution)/shard_map/ppermute | solution.py:25
  37.3 2.3 %shard_map.49 = (f32[512,256]{1,0:T(8,128)S(1)}, f32[512,128]{1,0:T(8,128)S(1)}) custom-call(s32[1]{0:T(128)} %bitcast.section_ref, f32[8,128]{1,0:T(8,128)S(1)} %collective-permute-done.flag_ref, bf16[512,256]{1,0:T(8,128)(2,1)S(1)} %bitcast.9, s32[512,128]{1,0:T(8,128)S(1)} %shard_map.46.columns_ref, f32[3,256]{1,0:T(4,128)S(1)} %copy-done, ...), custom_call_target="tpu_custom_call" | custom-call | flops 1073741824 | bytes 1048576 | tf_op jit(solution)/shard_map/pallas_call | solution.py:164
  39.7 0.9 %shard_map.51 = bf16[512,256]{1,0:T(8,128)(2,1)} custom-call(s32[1]{0:T(128)} %bitcast.section_ref, s32[512,128]{1,0:T(8,128)S(1)} %shard_map.46.columns_ref, f32[3,256]{1,0:T(4,128)S(1)} %copy-done, f32[512,256]{1,0:T(8,128)S(1)} %get-tuple-element.11.numerator_ref, f32[512,128]{1,0:T(8,128)S(1)} %get-tuple-element.12.count_ref, ...), custom_call_target="tpu_custom_call" | custom-call | tf_op jit(solution)/shard_map/pallas_call | solution.py:164
  (13 shorter events, 0.1 us)
Async XLA Ops:
  0.0 8.3 %collective-permute-start.2 = (bf16[512,256]{1,0:T(8,128)(2,1)}, bf16[512,256]{1,0:T(8,128)(2,1)S(1)}, u32[]{:S(2)}, u32[]{:S(2)}) collective-permute-start(bf16[512,256]{1,0:T(8,128)(2,1)} %bitcast.5), channel_id=1, source_target_pairs={{24,0},{28,4},{0,8},{4,12},{8,16},{12,20},{16,24},{20,28},{25,1},{... | collective-permute-start | bytes 786440 | tf_op jit(solution)/shard_map/ppermute | solution.py:25
  1.6 13.3 %collective-permute-start.7 = (bf16[512,256]{1,0:T(8,128)(2,1)}, bf16[512,256]{1,0:T(8,128)(2,1)S(1)}, u32[]{:S(2)}, u32[]{:S(2)}) collective-permute-start(bf16[512,256]{1,0:T(8,128)(2,1)} %bitcast.6), channel_id=1, source_target_pairs={{4,8},{12,16},{20,24},{8,4},{16,12},{24,20},{5,9},{13,17},{21,25},... | collective-permute-start | bytes 786440 | tf_op jit(solution)/shard_map/ppermute | solution.py:30
  4.9 13.4 %collective-permute-start.6 = (bf16[512,256]{1,0:T(8,128)(2,1)}, bf16[512,256]{1,0:T(8,128)(2,1)S(1)}, u32[]{:S(2)}, u32[]{:S(2)}) collective-permute-start(bf16[512,256]{1,0:T(8,128)(2,1)} %bitcast.7), channel_id=1, source_target_pairs={{0,4},{8,12},{16,20},{24,28},{4,0},{12,8},{20,16},{28,24},{1,5},{9... | collective-permute-start | bytes 786440 | tf_op jit(solution)/shard_map/ppermute | solution.py:30
  8.3 10.6 %collective-permute-start.3 = (bf16[512,256]{1,0:T(8,128)(2,1)S(1)}, bf16[512,256]{1,0:T(8,128)(2,1)S(1)}, u32[]{:S(2)}, u32[]{:S(2)}) collective-permute-start(bf16[512,256]{1,0:T(8,128)(2,1)S(1)} %collective-permute-done.2.refs_0_), channel_id=1, source_target_pairs={{2,0},{3,1},{0,2},{1,3},{6,4},{7,5},{4,6},{5,7},{10,8},{11,9},{8,1... | collective-permute-start | bytes 786440 | tf_op jit(solution)/shard_map/ppermute | solution.py:35
  18.3 7.0 %collective-permute-start.8 = (bf16[512,256]{1,0:T(8,128)(2,1)S(1)}, bf16[512,256]{1,0:T(8,128)(2,1)S(1)}, u32[]{:S(2)}, u32[]{:S(2)}) collective-permute-start(bf16[512,256]{1,0:T(8,128)(2,1)S(1)} %broadcast_select_fusion.refs_2_), channel_id=1, source_target_pairs={{2,0},{3,1},{0,2},{1,3},{6,4},{7,5},{4,6},{5,7},{10,8},{11,9},{8,1... | collective-permute-start | bytes 786440 | tf_op jit(solution)/shard_map/ppermute | solution.py:35
  18.8 6.5 %collective-permute-start.4 = (bf16[512,256]{1,0:T(8,128)(2,1)S(1)}, bf16[512,256]{1,0:T(8,128)(2,1)S(1)}, u32[]{:S(2)}, u32[]{:S(2)}) collective-permute-start(bf16[512,256]{1,0:T(8,128)(2,1)S(1)} %collective-permute-done.2.refs_0_), channel_id=1, source_target_pairs={{1,0},{0,1},{3,2},{2,3},{5,4},{4,5},{7,6},{6,7},{9,8},{8,9},{11,10... | collective-permute-start | bytes 786440 | tf_op jit(solution)/shard_map/ppermute | solution.py:35
  18.9 6.5 %collective-permute-start.5 = (bf16[512,256]{1,0:T(8,128)(2,1)S(1)}, bf16[512,256]{1,0:T(8,128)(2,1)S(1)}, u32[]{:S(2)}, u32[]{:S(2)}) collective-permute-start(bf16[512,256]{1,0:T(8,128)(2,1)S(1)} %collective-permute-done.3.refs_1_), channel_id=1, source_target_pairs={{1,0},{0,1},{3,2},{2,3},{5,4},{4,5},{7,6},{6,7},{9,8},{8,9},{11,10... | collective-permute-start | bytes 786440 | tf_op jit(solution)/shard_map/ppermute | solution.py:35
  20.1 5.2 %collective-permute-start.1 = (f32[8,128]{1,0:T(8,128)S(1)}, f32[8,128]{1,0:T(8,128)S(1)}, u32[]{:S(2)}, u32[]{:S(2)}) collective-permute-start(f32[8,128]{1,0:T(8,128)S(1)} %shard_map.47), channel_id=1, source_target_pairs={{24,0},{28,4},{0,8},{4,12},{8,16},{12,20},{16,24},{20,28},{25,1},{... | collective-permute-start | bytes 12296 | tf_op jit(solution)/shard_map/ppermute | solution.py:25
  21.7 15.6 %collective-permute-start.9 = (bf16[512,256]{1,0:T(8,128)(2,1)S(1)}, bf16[512,256]{1,0:T(8,128)(2,1)S(1)}, u32[]{:S(2)}, u32[]{:S(2)}) collective-permute-start(bf16[512,256]{1,0:T(8,128)(2,1)S(1)} %broadcast_select_fusion.refs_2_), channel_id=1, source_target_pairs={{1,0},{0,1},{3,2},{2,3},{5,4},{4,5},{7,6},{6,7},{9,8},{8,9},{11,10... | collective-permute-start | bytes 786440 | tf_op jit(solution)/shard_map/ppermute | solution.py:35
  25.3 12.0 %collective-permute-start.10 = (bf16[512,256]{1,0:T(8,128)(2,1)S(1)}, bf16[512,256]{1,0:T(8,128)(2,1)S(1)}, u32[]{:S(2)}, u32[]{:S(2)}) collective-permute-start(bf16[512,256]{1,0:T(8,128)(2,1)S(1)} %collective-permute-done.8.refs_3_), channel_id=1, source_target_pairs={{1,0},{0,1},{3,2},{2,3},{5,4},{4,5},{7,6},{6,7},{9,8},{8,9},{11,10... | collective-permute-start | bytes 786440 | tf_op jit(solution)/shard_map/ppermute | solution.py:35
  25.3 5.3 %copy-start.1 = (s32[1,512]{1,0:T(1,128)S(1)}, s32[1,512]{1,0:T(1,128)}, u32[]{:S(2)}) copy-start(s32[1,512]{1,0:T(1,128)} %select_ref.1) | copy-start | bytes 6148
  25.3 5.5 %copy-start.2 = (bf16[1,512,256]{2,1,0:T(8,128)(2,1)S(1)}, bf16[1,512,256]{2,1,0:T(8,128)(2,1)}, u32[]{:S(2)}) copy-start(bf16[1,512,256]{2,1,0:T(8,128)(2,1)} %param.4) | copy-start | bytes 786436
  27.5 3.3 %copy-start = (f32[3,256]{1,0:T(4,128)S(1)}, f32[3,256]{1,0:T(4,128)}, u32[]{:S(2)}) copy-start(f32[3,256]{1,0:T(4,128)} %gain_ref.5) | copy-start | bytes 9220
  27.6 12.1 %collective-permute-start.11 = (bf16[512,256]{1,0:T(8,128)(2,1)S(1)}, bf16[512,256]{1,0:T(8,128)(2,1)S(1)}, u32[]{:S(2)}, u32[]{:S(2)}) collective-permute-start(bf16[512,256]{1,0:T(8,128)(2,1)S(1)} %shard_map.50), channel_id=1, source_target_pairs={{8,12},{12,16},{16,20},{20,24},{24,28},{0,8},{4,0},{28,4},{9,13},{... | collective-permute-start | bytes 786440 | tf_op jit(solution)/shard_map/ppermute | solution.py:203
  28.0 9.3 %collective-permute-start = (f32[8,128]{1,0:T(8,128)S(1)}, f32[8,128]{1,0:T(8,128)S(1)}, u32[]{:S(2)}, u32[]{:S(2)}) collective-permute-start(f32[8,128]{1,0:T(8,128)S(1)} %shard_map.47), channel_id=1, source_target_pairs={{28,0},{0,4},{4,8},{8,12},{12,16},{16,20},{20,24},{24,28},{29,1},{... | collective-permute-start | bytes 12296 | tf_op jit(solution)/shard_map/ppermute | solution.py:25

commit v5 on v4

--- a/solution.py
+++ b/solution.py
@@ -44,24 +44,33 @@
     return jnp.where(mark <= usable_limit, 1.0, 0.0)
 
 
-def matched(queries, key_refs, scale):
+def matched(query_rows, key_refs, scale, num_rows):
     step = scale * math.log2(math.e)
-    scores = [
-        lax.dot_general(
-            queries, k[...], (((1,), (1,)), ((), ())), preferred_element_type=jnp.float32
-        )
-        for k in key_refs
-    ]
-    top = functools.reduce(jnp.maximum, [s.max(axis=1, keepdims=True) for s in scores]) * step
-    total = 0.0
-    weighted = 0.0
-    for s, k in zip(scores, key_refs):
-        weights = jnp.exp2(s * step - top)
-        total = total + jnp.sum(weights, axis=1, keepdims=True)
-        weighted = weighted + jnp.dot(
-            weights.astype(jnp.bfloat16), k[...], preferred_element_type=jnp.float32
-        )
-    return weighted, total
+    blocks = [slice(row, row + row_block) for row in range(0, num_rows, row_block)]
+
+    def scored(rows):
+        queries = query_rows(rows)
+        return [
+            lax.dot_general(
+                queries, k[...], (((1,), (1,)), ((), ())), preferred_element_type=jnp.float32
+            )
+            for k in key_refs
+        ]
+
+    scores = scored(blocks[0])
+    for rows, rows_after in zip(blocks, blocks[1:] + [None]):
+        scores_after = None if rows_after is None else scored(rows_after)
+        top = functools.reduce(jnp.maximum, [s.max(axis=1, keepdims=True) for s in scores]) * step
+        total = 0.0
+        weighted = 0.0
+        for s, k in zip(scores, key_refs):
+            weights = jnp.exp2(s * step - top)
+            total = total + jnp.sum(weights, axis=1, keepdims=True)
+            weighted = weighted + jnp.dot(
+                weights.astype(jnp.bfloat16), k[...], preferred_element_type=jnp.float32
+            )
+        yield rows, weighted, total
+        scores = scores_after
 
 
 def chosen_rows(columns, offset, section_ref, usable):
@@ -88,10 +97,11 @@
     @pl.when(needed)
     def _():
         keep = jnp.broadcast_to(widen(flag_ref[0:1, :], channels), (row_block, channels)) > 0.5
-        for row in range(0, num_rows, row_block):
-            rows = slice(row, row + row_block)
-            queries = jnp.where(section % 2 == 1, across_ref[rows, :], beside_ref[rows, :])
-            weighted, total = matched(queries, key_refs, scale)
+
+        def queries(rows):
+            return jnp.where(section % 2 == 1, across_ref[rows, :], beside_ref[rows, :])
+
+        for rows, weighted, total in matched(queries, key_refs, scale, num_rows):
             out_ref[rows, :] = jnp.where(keep, weighted / total, unusable).astype(jnp.bfloat16)
 
     @pl.when(jnp.logical_not(needed))
@@ -110,9 +120,7 @@
 
     @pl.when(needed)
     def _():
-        for row in range(0, num_rows, row_block):
-            rows = slice(row, row + row_block)
-            weighted, total = matched(query_ref[rows, :], key_refs, scale)
+        for rows, weighted, total in matched(lambda r: query_ref[r, :], key_refs, scale, num_rows):
             count = chosen_rows(columns_ref[rows, :], offset, section_ref, usable)
             numerator = weighted * widen(count / total, channels) * gain
             if not first:

time: 40.7 us -> 39.7 us (0.975)
  the two profiles are of different devices: /device:TPU:20 before, /device:TPU:0 now
where the time goes in v5:
time: 39.7 us; the launch traced here: 39.3 us
  waiting for transfers between devices  20.7 us (52%)
  starting transfers between devices  16.6 us (42%)
  Pallas kernels  1.23 us (3%)
  between operations  0.75 us (2%)
    ppermute x3, waiting for transfers between devices, from_behind(): lax.ppermute(block, 'sec', [((i - distance) % n, i) for i in range(n)])  14.3 us
    ppermute x3, starting transfers between devices, from_behind(): lax.ppermute(block, 'sec', [((i - distance) % n, i) for i in range(n)])  5.39 us
    ppermute x2, starting transfers between devices, swapped(): return lax.ppermute(block, 'sec', pairs + [(j, i) for i, j in pairs])  5 us
    ppermute x2, waiting for transfers between devices, swapped(): return lax.ppermute(block, 'sec', pairs + [(j, i) for i, j in pairs])  4.78 us
    ppermute x6, starting transfers between devices, from_partner(): return lax.ppermute(block, 'tile', [(i ^ distance, i) for i in range(n)])  3.84 us
    ppermute x1, starting transfers between devices, shards(): third = lax.ppermute(answered, 'sec', routes)  2.33 us
    ppermute x6, waiting for transfers between devices, from_partner(): return lax.ppermute(block, 'tile', [(i ^ distance, i) for i in range(n)])  1.59 us
    pallas_call x6, Pallas kernels, call(): pl.pallas_call(body, out_shape=out, in_specs=[smem] * scalars + [vmem] *...  1.23 us
  transfers between devices with their start and end apart: 12, of which 5 were waited for; matrix products, arithmetic and copies ran while one was open for 0% of the time, Pallas kernels for 1%

profile of v5, /device:TPU:0, one launch (start us, length us, event | category | flops | bytes accessed | tf_op | source)
XLA Modules:
  0.0 39.3 jit_solution(15576575824601608956)
XLA Ops:
  0.0 3.1 %collective-permute-start.2 = (bf16[512,256]{1,0:T(8,128)(2,1)}, bf16[512,256]{1,0:T(8,128)(2,1)S(1)}, u32[]{:S(2)}, u32[]{:S(2)}) collective-permute-start(bf16[512,256]{1,0:T(8,128)(2,1)} %bitcast.5), channel_id=1, source_target_pairs={{24,0},{28,4},{0,8},{4,12},{8,16},{12,20},{16,24},{20,28},{25,1},{... | collective-permute-start | bytes 786440 | tf_op jit(solution)/shard_map/ppermute | solution.py:25
  3.1 0.7 %collective-permute-start.7 = (bf16[512,256]{1,0:T(8,128)(2,1)}, bf16[512,256]{1,0:T(8,128)(2,1)S(1)}, u32[]{:S(2)}, u32[]{:S(2)}) collective-permute-start(bf16[512,256]{1,0:T(8,128)(2,1)} %bitcast.6), channel_id=1, source_target_pairs={{4,8},{12,16},{20,24},{8,4},{16,12},{24,20},{5,9},{13,17},{21,25},... | collective-permute-start | bytes 786440 | tf_op jit(solution)/shard_map/ppermute | solution.py:30
  3.7 4.3 %collective-permute-start.6 = (bf16[512,256]{1,0:T(8,128)(2,1)}, bf16[512,256]{1,0:T(8,128)(2,1)S(1)}, u32[]{:S(2)}, u32[]{:S(2)}) collective-permute-start(bf16[512,256]{1,0:T(8,128)(2,1)} %bitcast.7), channel_id=1, source_target_pairs={{0,4},{8,12},{16,20},{24,28},{4,0},{12,8},{20,16},{28,24},{1,5},{9... | collective-permute-start | bytes 786440 | tf_op jit(solution)/shard_map/ppermute | solution.py:30
  8.1 4.4 %collective-permute-done.2.refs_0_ = bf16[512,256]{1,0:T(8,128)(2,1)S(1)} collective-permute-done((bf16[512,256]{1,0:T(8,128)(2,1)}, bf16[512,256]{1,0:T(8,128)(2,1)S(1)}, u32[]{:S(2)}, u32[]{:S(2)}) %collective-permute-start.2) | collective-permute-done | bytes 262176 | tf_op jit(solution)/shard_map/ppermute | solution.py:25
  12.4 1.7 %collective-permute-start.3 = (bf16[512,256]{1,0:T(8,128)(2,1)S(1)}, bf16[512,256]{1,0:T(8,128)(2,1)S(1)}, u32[]{:S(2)}, u32[]{:S(2)}) collective-permute-start(bf16[512,256]{1,0:T(8,128)(2,1)S(1)} %collective-permute-done.2.refs_0_), channel_id=1, source_target_pairs={{2,0},{3,1},{0,2},{1,3},{6,4},{7,5},{4,6},{5,7},{10,8},{11,9},{8,1... | collective-permute-start | bytes 786440 | tf_op jit(solution)/shard_map/ppermute | solution.py:35
  14.2 0.0 collective-permute-done.7.across_ref
  14.2 4.8 %collective-permute-done.6.beside_ref = bf16[512,256]{1,0:T(8,128)(2,1)S(1)} collective-permute-done((bf16[512,256]{1,0:T(8,128)(2,1)}, bf16[512,256]{1,0:T(8,128)(2,1)S(1)}, u32[]{:S(2)}, u32[]{:S(2)}) %collective-permute-start.6) | collective-permute-done | bytes 262176 | tf_op jit(solution)/shard_map/ppermute | solution.py:30
  19.0 1.6 %collective-permute-start.8 = (bf16[512,256]{1,0:T(8,128)(2,1)S(1)}, bf16[512,256]{1,0:T(8,128)(2,1)S(1)}, u32[]{:S(2)}, u32[]{:S(2)}) collective-permute-start(bf16[512,256]{1,0:T(8,128)(2,1)S(1)} %broadcast_select_fusion.refs_2_), channel_id=1, source_target_pairs={{2,0},{3,1},{0,2},{1,3},{6,4},{7,5},{4,6},{5,7},{10,8},{11,9},{8,1... | collective-permute-start | bytes 786440 | tf_op jit(solution)/shard_map/ppermute | solution.py:35
  20.6 0.5 %collective-permute-start.5 = (bf16[512,256]{1,0:T(8,128)(2,1)S(1)}, bf16[512,256]{1,0:T(8,128)(2,1)S(1)}, u32[]{:S(2)}, u32[]{:S(2)}) collective-permute-start(bf16[512,256]{1,0:T(8,128)(2,1)S(1)} %collective-permute-done.3.refs_1_), channel_id=1, source_target_pairs={{1,0},{0,1},{3,2},{2,3},{5,4},{4,5},{7,6},{6,7},{9,8},{8,9},{11,10... | collective-permute-start | bytes 786440 | tf_op jit(solution)/shard_map/ppermute | solution.py:35
  21.7 0.1 shard_map.47
  21.8 2.3 %collective-permute-start.1 = (f32[8,128]{1,0:T(8,128)S(1)}, f32[8,128]{1,0:T(8,128)S(1)}, u32[]{:S(2)}, u32[]{:S(2)}) collective-permute-start(f32[8,128]{1,0:T(8,128)S(1)} %shard_map.47), channel_id=1, source_target_pairs={{24,0},{28,4},{0,8},{4,12},{8,16},{12,20},{16,24},{20,28},{25,1},{... | collective-permute-start | bytes 12296 | tf_op jit(solution)/shard_map/ppermute | solution.py:25
  24.2 0.0 collective-permute-start.9
  24.2 1.6 %collective-permute-done.8.refs_3_ = bf16[512,256]{1,0:T(8,128)(2,1)S(1)} collective-permute-done((bf16[512,256]{1,0:T(8,128)(2,1)S(1)}, bf16[512,256]{1,0:T(8,128)(2,1)S(1)}, u32[]{:S(2)}, u32[]{:S(2)}) %collective-permute-start.8) | collective-permute-done | bytes 262176 | tf_op jit(solution)/shard_map/ppermute | solution.py:35
  25.7 2.0 %collective-permute-done.1.flag_ref = f32[8,128]{1,0:T(8,128)S(1)} collective-permute-done((f32[8,128]{1,0:T(8,128)S(1)}, f32[8,128]{1,0:T(8,128)S(1)}, u32[]{:S(2)}, u32[]{:S(2)}) %collective-permute-start.1) | collective-permute-done | bytes 4128 | tf_op jit(solution)/shard_map/ppermute | solution.py:25
  27.8 0.0 collective-permute-done.4.refs_2_
  27.8 0.0 collective-permute-done.5.refs_3_
  27.8 0.0 copy-start.2
  27.8 0.0 copy-start
  27.8 2.3 %collective-permute-start.11 = (bf16[512,256]{1,0:T(8,128)(2,1)S(1)}, bf16[512,256]{1,0:T(8,128)(2,1)S(1)}, u32[]{:S(2)}, u32[]{:S(2)}) collective-permute-start(bf16[512,256]{1,0:T(8,128)(2,1)S(1)} %shard_map.50), channel_id=1, source_target_pairs={{8,12},{12,16},{16,20},{20,24},{24,28},{0,8},{4,0},{28,4},{9,13},{... | collective-permute-start | bytes 786440 | tf_op jit(solution)/shard_map/ppermute | solution.py:211
  30.2 0.1 shard_map.46.columns_ref
  30.3 0.1 shard_map.48
  30.4 7.9 %collective-permute-done.flag_ref = f32[8,128]{1,0:T(8,128)S(1)} collective-permute-done((f32[8,128]{1,0:T(8,128)S(1)}, f32[8,128]{1,0:T(8,128)S(1)}, u32[]{:S(2)}, u32[]{:S(2)}) %collective-permute-start) | collective-permute-done | bytes 4128 | tf_op jit(solution)/shard_map/ppermute | solution.py:25
  38.3 0.1 shard_map.49
  38.4 0.9 %shard_map.51 = bf16[512,256]{1,0:T(8,128)(2,1)} custom-call(s32[1]{0:T(128)} %bitcast.section_ref, s32[512,128]{1,0:T(8,128)S(1)} %shard_map.46.columns_ref, f32[3,256]{1,0:T(4,128)S(1)} %copy-done, f32[512,256]{1,0:T(8,128)S(1)} %get-tuple-element.11.numerator_ref, f32[512,128]{1,0:T(8,128)S(1)} %get-tuple-element.12.count_ref, ...), custom_call_target="tpu_custom_call" | custom-call | tf_op jit(solution)/shard_map/pallas_call | solution.py:172
  (13 shorter events, 0.1 us)
Async XLA Ops:
  0.0 12.4 %collective-permute-start.2 = (bf16[512,256]{1,0:T(8,128)(2,1)}, bf16[512,256]{1,0:T(8,128)(2,1)S(1)}, u32[]{:S(2)}, u32[]{:S(2)}) collective-permute-start(bf16[512,256]{1,0:T(8,128)(2,1)} %bitcast.5), channel_id=1, source_target_pairs={{24,0},{28,4},{0,8},{4,12},{8,16},{12,20},{16,24},{20,28},{25,1},{... | collective-permute-start | bytes 786440 | tf_op jit(solution)/shard_map/ppermute | solution.py:25
  3.1 11.1 %collective-permute-start.7 = (bf16[512,256]{1,0:T(8,128)(2,1)}, bf16[512,256]{1,0:T(8,128)(2,1)S(1)}, u32[]{:S(2)}, u32[]{:S(2)}) collective-permute-start(bf16[512,256]{1,0:T(8,128)(2,1)} %bitcast.6), channel_id=1, source_target_pairs={{4,8},{12,16},{20,24},{8,4},{16,12},{24,20},{5,9},{13,17},{21,25},... | collective-permute-start | bytes 786440 | tf_op jit(solution)/shard_map/ppermute | solution.py:30
  3.7 15.2 %collective-permute-start.6 = (bf16[512,256]{1,0:T(8,128)(2,1)}, bf16[512,256]{1,0:T(8,128)(2,1)S(1)}, u32[]{:S(2)}, u32[]{:S(2)}) collective-permute-start(bf16[512,256]{1,0:T(8,128)(2,1)} %bitcast.7), channel_id=1, source_target_pairs={{0,4},{8,12},{16,20},{24,28},{4,0},{12,8},{20,16},{28,24},{1,5},{9... | collective-permute-start | bytes 786440 | tf_op jit(solution)/shard_map/ppermute | solution.py:30
  12.4 8.1 %collective-permute-start.3 = (bf16[512,256]{1,0:T(8,128)(2,1)S(1)}, bf16[512,256]{1,0:T(8,128)(2,1)S(1)}, u32[]{:S(2)}, u32[]{:S(2)}) collective-permute-start(bf16[512,256]{1,0:T(8,128)(2,1)S(1)} %collective-permute-done.2.refs_0_), channel_id=1, source_target_pairs={{2,0},{3,1},{0,2},{1,3},{6,4},{7,5},{4,6},{5,7},{10,8},{11,9},{8,1... | collective-permute-start | bytes 786440 | tf_op jit(solution)/shard_map/ppermute | solution.py:35
  19.0 6.7 %collective-permute-start.8 = (bf16[512,256]{1,0:T(8,128)(2,1)S(1)}, bf16[512,256]{1,0:T(8,128)(2,1)S(1)}, u32[]{:S(2)}, u32[]{:S(2)}) collective-permute-start(bf16[512,256]{1,0:T(8,128)(2,1)S(1)} %broadcast_select_fusion.refs_2_), channel_id=1, source_target_pairs={{2,0},{3,1},{0,2},{1,3},{6,4},{7,5},{4,6},{5,7},{10,8},{11,9},{8,1... | collective-permute-start | bytes 786440 | tf_op jit(solution)/shard_map/ppermute | solution.py:35
  20.6 7.2 %collective-permute-start.4 = (bf16[512,256]{1,0:T(8,128)(2,1)S(1)}, bf16[512,256]{1,0:T(8,128)(2,1)S(1)}, u32[]{:S(2)}, u32[]{:S(2)}) collective-permute-start(bf16[512,256]{1,0:T(8,128)(2,1)S(1)} %collective-permute-done.2.refs_0_), channel_id=1, source_target_pairs={{1,0},{0,1},{3,2},{2,3},{5,4},{4,5},{7,6},{6,7},{9,8},{8,9},{11,10... | collective-permute-start | bytes 786440 | tf_op jit(solution)/shard_map/ppermute | solution.py:35
  20.6 7.2 %collective-permute-start.5 = (bf16[512,256]{1,0:T(8,128)(2,1)S(1)}, bf16[512,256]{1,0:T(8,128)(2,1)S(1)}, u32[]{:S(2)}, u32[]{:S(2)}) collective-permute-start(bf16[512,256]{1,0:T(8,128)(2,1)S(1)} %collective-permute-done.3.refs_1_), channel_id=1, source_target_pairs={{1,0},{0,1},{3,2},{2,3},{5,4},{4,5},{7,6},{6,7},{9,8},{8,9},{11,10... | collective-permute-start | bytes 786440 | tf_op jit(solution)/shard_map/ppermute | solution.py:35
  21.8 5.9 %collective-permute-start.1 = (f32[8,128]{1,0:T(8,128)S(1)}, f32[8,128]{1,0:T(8,128)S(1)}, u32[]{:S(2)}, u32[]{:S(2)}) collective-permute-start(f32[8,128]{1,0:T(8,128)S(1)} %shard_map.47), channel_id=1, source_target_pairs={{24,0},{28,4},{0,8},{4,12},{8,16},{12,20},{16,24},{20,28},{25,1},{... | collective-permute-start | bytes 12296 | tf_op jit(solution)/shard_map/ppermute | solution.py:25
  24.2 14.1 %collective-permute-start.9 = (bf16[512,256]{1,0:T(8,128)(2,1)S(1)}, bf16[512,256]{1,0:T(8,128)(2,1)S(1)}, u32[]{:S(2)}, u32[]{:S(2)}) collective-permute-start(bf16[512,256]{1,0:T(8,128)(2,1)S(1)} %broadcast_select_fusion.refs_2_), channel_id=1, source_target_pairs={{1,0},{0,1},{3,2},{2,3},{5,4},{4,5},{7,6},{6,7},{9,8},{8,9},{11,10... | collective-permute-start | bytes 786440 | tf_op jit(solution)/shard_map/ppermute | solution.py:35
  25.7 12.6 %collective-permute-start.10 = (bf16[512,256]{1,0:T(8,128)(2,1)S(1)}, bf16[512,256]{1,0:T(8,128)(2,1)S(1)}, u32[]{:S(2)}, u32[]{:S(2)}) collective-permute-start(bf16[512,256]{1,0:T(8,128)(2,1)S(1)} %collective-permute-done.8.refs_3_), channel_id=1, source_target_pairs={{1,0},{0,1},{3,2},{2,3},{5,4},{4,5},{7,6},{6,7},{9,8},{8,9},{11,10... | collective-permute-start | bytes 786440 | tf_op jit(solution)/shard_map/ppermute | solution.py:35
  27.8 2.4 %copy-start.1 = (s32[1,512]{1,0:T(1,128)S(1)}, s32[1,512]{1,0:T(1,128)}, u32[]{:S(2)}) copy-start(s32[1,512]{1,0:T(1,128)} %select_ref.1) | copy-start | bytes 6148
  27.8 2.5 %copy-start.2 = (bf16[1,512,256]{2,1,0:T(8,128)(2,1)S(1)}, bf16[1,512,256]{2,1,0:T(8,128)(2,1)}, u32[]{:S(2)}) copy-start(bf16[1,512,256]{2,1,0:T(8,128)(2,1)} %param.4) | copy-start | bytes 786436
  27.8 2.5 %copy-start = (f32[3,256]{1,0:T(4,128)S(1)}, f32[3,256]{1,0:T(4,128)}, u32[]{:S(2)}) copy-start(f32[3,256]{1,0:T(4,128)} %gain_ref.5) | copy-start | bytes 9220
  27.8 10.5 %collective-permute-start.11 = (bf16[512,256]{1,0:T(8,128)(2,1)S(1)}, bf16[512,256]{1,0:T(8,128)(2,1)S(1)}, u32[]{:S(2)}, u32[]{:S(2)}) collective-permute-start(bf16[512,256]{1,0:T(8,128)(2,1)S(1)} %shard_map.50), channel_id=1, source_target_pairs={{8,12},{12,16},{16,20},{20,24},{24,28},{0,8},{4,0},{28,4},{9,13},{... | collective-permute-start | bytes 786440 | tf_op jit(solution)/shard_map/ppermute | solution.py:211
  30.2 8.1 %collective-permute-start = (f32[8,128]{1,0:T(8,128)S(1)}, f32[8,128]{1,0:T(8,128)S(1)}, u32[]{:S(2)}, u32[]{:S(2)}) collective-permute-start(f32[8,128]{1,0:T(8,128)S(1)} %shard_map.47), channel_id=1, source_target_pairs={{28,0},{0,4},{4,8},{8,12},{12,16},{16,20},{20,24},{24,28},{29,1},{... | collective-permute-start | bytes 12296 | tf_op jit(solution)/shard_map/ppermute | solution.py:25

commit v6 on v5

--- a/solution.py
+++ b/solution.py
@@ -25,9 +25,30 @@
     return lax.ppermute(block, "sec", [((i - distance) % n, i) for i in range(n)])
 
 
+def over_both(block, route):
+    n, tiles = lax.axis_size("sec"), lax.axis_size("tile")
+    pairs = []
+    for i in range(n):
+        for t in range(tiles):
+            to_section, to_tile = route(i, t, n)
+            pairs.append((i * tiles + t, to_section * tiles + to_tile))
+    return lax.ppermute(block, ("sec", "tile"), pairs)
+
+
+def up_and_down(block, parity):
+    def route(i, t, n):
+        to = i + 2 if t % 2 == parity else i - 2
+        return (to, t) if 0 <= to < n else (i, t ^ 1)
+
+    return over_both(block, route)
+
+
 def swapped(block, first):
-    pairs = [(i, i + 1) for i in range(first, lax.axis_size("sec") - 1, 2)]
-    return lax.ppermute(block, "sec", pairs + [(j, i) for i, j in pairs])
+    def route(i, t, n):
+        to = i + 1 if i % 2 == first else i - 1
+        return (to, t) if 0 <= to < n else (i, t ^ 1)
+
+    return over_both(block, route)
 
 
 def from_partner(block, distance):
@@ -191,7 +212,9 @@
     mark_shape = jax.ShapeDtypeStruct((sublanes, lanes), jnp.float32)
     columns = call(prepare, columns_shape, (select,))
     mark = call(note, mark_shape, (validity[:, None],))
-    second = from_behind(queries, 2)
+    even_up = up_and_down(queries, 0)
+    odd_up = up_and_down(queries, 1)
+    second = jnp.where(lax.axis_index("tile") % 2 == 0, even_up, odd_up)
     beside = swapped(queries, 0)
     across = swapped(queries, 1)
     flag1 = from_behind(mark, 1)

time: 39.7 us -> 38 us (0.957)
  starting transfers between devices: 16.6 us -> 10.4 us
  waiting for transfers between devices: 20.7 us -> 25.3 us
    ppermute x2 -> x4, waiting for transfers between devices: 4.78 us -> 9.7 us  [over_both(): return lax.ppermute(block, ('sec', 'tile'), pairs)]
    ppermute x3 -> x2, waiting for transfers between devices: 14.3 us -> 10 us  [from_behind(): lax.ppermute(block, 'sec', [((i - distance) % n, i) for i in range(n)])]
    ppermute x6, waiting for transfers between devices: 1.59 us -> 5.61 us  [from_partner(): return lax.ppermute(block, 'tile', [(i ^ distance, i) for i in range(n)])]
    ppermute x3 -> x2, starting transfers between devices: 5.39 us -> 1.42 us  [from_behind(): lax.ppermute(block, 'sec', [((i - distance) % n, i) for i in range(n)])]
    ppermute x1, starting transfers between devices: 2.33 us -> 0.99 us  [shards(): third = lax.ppermute(answered, 'sec', routes)]
    ppermute x2 -> x4, starting transfers between devices: 5 us -> 4.55 us  [over_both(): return lax.ppermute(block, ('sec', 'tile'), pairs)]
  transfers between devices with their start and end apart: 12 -> 13, of which waited for: 5 -> 7; matrix products, arithmetic and copies ran while one was open for 0% -> 0% of each run, Pallas kernels for 1% -> 1%
where the time goes in v6:
time: 38 us; the launch traced here: 37.8 us
  waiting for transfers between devices  25.3 us (67%)
  starting transfers between devices  10.4 us (27%)
  Pallas kernels  1.23 us (3%)
  between operations  0.75 us (2%)
    ppermute x2, waiting for transfers between devices, from_behind(): lax.ppermute(block, 'sec', [((i - distance) % n, i) for i in range(n)])  10 us
    ppermute x4, waiting for transfers between devices, over_both(): return lax.ppermute(block, ('sec', 'tile'), pairs)  9.7 us
    ppermute x6, waiting for transfers between devices, from_partner(): return lax.ppermute(block, 'tile', [(i ^ distance, i) for i in range(n)])  5.61 us
    ppermute x4, starting transfers between devices, over_both(): return lax.ppermute(block, ('sec', 'tile'), pairs)  4.55 us
    ppermute x6, starting transfers between devices, from_partner(): return lax.ppermute(block, 'tile', [(i ^ distance, i) for i in range(n)])  3.49 us
    ppermute x2, starting transfers between devices, from_behind(): lax.ppermute(block, 'sec', [((i - distance) % n, i) for i in range(n)])  1.42 us
    pallas_call x6, Pallas kernels, call(): pl.pallas_call(body, out_shape=out, in_specs=[smem] * scalars + [vmem] *...  1.23 us
    ppermute x1, starting transfers between devices, shards(): third = lax.ppermute(answered, 'sec', routes)  0.99 us
  transfers between devices with their start and end apart: 13, of which 7 were waited for; matrix products, arithmetic and copies ran while one was open for 0% of the time, Pallas kernels for 1%

profile of v6, /device:TPU:0, one launch (start us, length us, event | category | flops | bytes accessed | tf_op | source)
XLA Modules:
  0.0 37.8 jit_solution(3349118692876458668)
XLA Ops:
  0.0 3.1 %collective-permute-start.2 = (bf16[512,256]{1,0:T(8,128)(2,1)}, bf16[512,256]{1,0:T(8,128)(2,1)S(1)}, u32[]{:S(2)}, u32[]{:S(2)}) collective-permute-start(bf16[512,256]{1,0:T(8,128)(2,1)} %bitcast.5), channel_id=1, source_target_pairs={{0,8},{1,0},{2,10},{3,2},{4,12},{5,4},{6,14},{7,6},{8,16},{9,1},{1... | collective-permute-start | bytes 786440 | tf_op jit(solution)/shard_map/ppermute | solution.py:35
  3.1 0.0 collective-permute-start.3
  3.1 1.5 %collective-permute-start.7 = (bf16[512,256]{1,0:T(8,128)(2,1)}, bf16[512,256]{1,0:T(8,128)(2,1)S(1)}, u32[]{:S(2)}, u32[]{:S(2)}) collective-permute-start(bf16[512,256]{1,0:T(8,128)(2,1)} %bitcast.7), channel_id=1, source_target_pairs={{0,4},{1,5},{2,6},{3,7},{4,0},{5,1},{6,2},{7,3},{8,12},{9,13},{10,... | collective-permute-start | bytes 786440 | tf_op jit(solution)/shard_map/ppermute | solution.py:35
  4.6 4.4 %collective-permute-done.2 = bf16[512,256]{1,0:T(8,128)(2,1)S(1)} collective-permute-done((bf16[512,256]{1,0:T(8,128)(2,1)}, bf16[512,256]{1,0:T(8,128)(2,1)S(1)}, u32[]{:S(2)}, u32[]{:S(2)}) %collective-permute-start.2) | collective-permute-done | bytes 262176 | tf_op jit(solution)/shard_map/ppermute | solution.py:35
  8.9 3.4 %collective-permute-done.3 = bf16[512,256]{1,0:T(8,128)(2,1)S(1)} collective-permute-done((bf16[512,256]{1,0:T(8,128)(2,1)}, bf16[512,256]{1,0:T(8,128)(2,1)S(1)}, u32[]{:S(2)}, u32[]{:S(2)}) %collective-permute-start.3) | collective-permute-done | bytes 262176 | tf_op jit(solution)/shard_map/ppermute | solution.py:35
  12.4 1.7 %collective-permute-start.4 = (bf16[512,256]{1,0:T(8,128)(2,1)S(1)}, bf16[512,256]{1,0:T(8,128)(2,1)S(1)}, u32[]{:S(2)}, u32[]{:S(2)}) collective-permute-start(bf16[512,256]{1,0:T(8,128)(2,1)S(1)} %broadcast_select_fusion.1.refs_0_), channel_id=1, source_target_pairs={{2,0},{3,1},{0,2},{1,3},{6,4},{7,5},{4,6},{5,7},{10,8},{11,9},{8,1... | collective-permute-start | bytes 786440 | tf_op jit(solution)/shard_map/ppermute | solution.py:56
  14.1 1.9 %collective-permute-done.7.beside_ref = bf16[512,256]{1,0:T(8,128)(2,1)S(1)} collective-permute-done((bf16[512,256]{1,0:T(8,128)(2,1)}, bf16[512,256]{1,0:T(8,128)(2,1)S(1)}, u32[]{:S(2)}, u32[]{:S(2)}) %collective-permute-start.7) | collective-permute-done | bytes 262176 | tf_op jit(solution)/shard_map/ppermute | solution.py:35
  15.9 0.0 collective-permute-done.8.across_ref
  16.0 1.6 %collective-permute-start.9 = (bf16[512,256]{1,0:T(8,128)(2,1)S(1)}, bf16[512,256]{1,0:T(8,128)(2,1)S(1)}, u32[]{:S(2)}, u32[]{:S(2)}) collective-permute-start(bf16[512,256]{1,0:T(8,128)(2,1)S(1)} %broadcast_select_fusion.refs_2_), channel_id=1, source_target_pairs={{2,0},{3,1},{0,2},{1,3},{6,4},{7,5},{4,6},{5,7},{10,8},{11,9},{8,1... | collective-permute-start | bytes 786440 | tf_op jit(solution)/shard_map/ppermute | solution.py:56
  17.6 3.2 %collective-permute-done.4.refs_1_ = bf16[512,256]{1,0:T(8,128)(2,1)S(1)} collective-permute-done((bf16[512,256]{1,0:T(8,128)(2,1)S(1)}, bf16[512,256]{1,0:T(8,128)(2,1)S(1)}, u32[]{:S(2)}, u32[]{:S(2)}) %collective-permute-start.4) | collective-permute-done | bytes 262176 | tf_op jit(solution)/shard_map/ppermute | solution.py:56
  21.4 0.1 shard_map.47
  21.5 0.3 collective-permute-start.1
  21.8 0.2 collective-permute-start.10
  22.0 2.4 %collective-permute-done.9.refs_3_ = bf16[512,256]{1,0:T(8,128)(2,1)S(1)} collective-permute-done((bf16[512,256]{1,0:T(8,128)(2,1)S(1)}, bf16[512,256]{1,0:T(8,128)(2,1)S(1)}, u32[]{:S(2)}, u32[]{:S(2)}) %collective-permute-start.9) | collective-permute-done | bytes 262176 | tf_op jit(solution)/shard_map/ppermute | solution.py:56
  24.5 2.4 %collective-permute-done.1.flag_ref = f32[8,128]{1,0:T(8,128)S(1)} collective-permute-done((f32[8,128]{1,0:T(8,128)S(1)}, f32[8,128]{1,0:T(8,128)S(1)}, u32[]{:S(2)}, u32[]{:S(2)}) %collective-permute-start.1) | collective-permute-done | bytes 4128 | tf_op jit(solution)/shard_map/ppermute | solution.py:25
  26.9 0.0 copy-start.2
  26.9 0.0 copy-start
  26.9 1.0 %collective-permute-start.12 = (bf16[512,256]{1,0:T(8,128)(2,1)S(1)}, bf16[512,256]{1,0:T(8,128)(2,1)S(1)}, u32[]{:S(2)}, u32[]{:S(2)}) collective-permute-start(bf16[512,256]{1,0:T(8,128)(2,1)S(1)} %shard_map.50), channel_id=1, source_target_pairs={{8,12},{12,16},{16,20},{20,24},{24,28},{0,8},{4,0},{28,4},{9,13},{... | collective-permute-start | bytes 786440 | tf_op jit(solution)/shard_map/ppermute | solution.py:234
  27.9 1.1 %collective-permute-start = (f32[8,128]{1,0:T(8,128)S(1)}, f32[8,128]{1,0:T(8,128)S(1)}, u32[]{:S(2)}, u32[]{:S(2)}) collective-permute-start(f32[8,128]{1,0:T(8,128)S(1)} %shard_map.47), channel_id=1, source_target_pairs={{28,0},{0,4},{4,8},{8,12},{12,16},{16,20},{20,24},{24,28},{29,1},{... | collective-permute-start | bytes 12296 | tf_op jit(solution)/shard_map/ppermute | solution.py:25
  29.0 0.1 shard_map.46.columns_ref
  29.2 0.1 shard_map.48
  29.3 7.6 %collective-permute-done.flag_ref = f32[8,128]{1,0:T(8,128)S(1)} collective-permute-done((f32[8,128]{1,0:T(8,128)S(1)}, f32[8,128]{1,0:T(8,128)S(1)}, u32[]{:S(2)}, u32[]{:S(2)}) %collective-permute-start) | collective-permute-done | bytes 4128 | tf_op jit(solution)/shard_map/ppermute | solution.py:25
  36.9 0.1 shard_map.49
  36.9 0.9 %shard_map.51 = bf16[512,256]{1,0:T(8,128)(2,1)} custom-call(s32[1]{0:T(128)} %bitcast.section_ref, s32[512,128]{1,0:T(8,128)S(1)} %shard_map.46.columns_ref, f32[3,256]{1,0:T(4,128)S(1)} %copy-done, f32[512,256]{1,0:T(8,128)S(1)} %get-tuple-element.11.numerator_ref, f32[512,128]{1,0:T(8,128)S(1)} %get-tuple-element.12.count_ref, ...), custom_call_target="tpu_custom_call" | custom-call | tf_op jit(solution)/shard_map/pallas_call | solution.py:193
  (16 shorter events, 0.1 us)
Async XLA Ops:
  0.0 8.9 %collective-permute-start.2 = (bf16[512,256]{1,0:T(8,128)(2,1)}, bf16[512,256]{1,0:T(8,128)(2,1)S(1)}, u32[]{:S(2)}, u32[]{:S(2)}) collective-permute-start(bf16[512,256]{1,0:T(8,128)(2,1)} %bitcast.5), channel_id=1, source_target_pairs={{0,8},{1,0},{2,10},{3,2},{4,12},{5,4},{6,14},{7,6},{8,16},{9,1},{1... | collective-permute-start | bytes 786440 | tf_op jit(solution)/shard_map/ppermute | solution.py:35
  3.1 9.3 %collective-permute-start.3 = (bf16[512,256]{1,0:T(8,128)(2,1)}, bf16[512,256]{1,0:T(8,128)(2,1)S(1)}, u32[]{:S(2)}, u32[]{:S(2)}) collective-permute-start(bf16[512,256]{1,0:T(8,128)(2,1)} %bitcast.6), channel_id=1, source_target_pairs={{0,1},{1,9},{2,3},{3,11},{4,5},{5,13},{6,7},{7,15},{8,0},{9,17},{1... | collective-permute-start | bytes 786440 | tf_op jit(solution)/shard_map/ppermute | solution.py:35
  3.1 12.9 %collective-permute-start.7 = (bf16[512,256]{1,0:T(8,128)(2,1)}, bf16[512,256]{1,0:T(8,128)(2,1)S(1)}, u32[]{:S(2)}, u32[]{:S(2)}) collective-permute-start(bf16[512,256]{1,0:T(8,128)(2,1)} %bitcast.7), channel_id=1, source_target_pairs={{0,4},{1,5},{2,6},{3,7},{4,0},{5,1},{6,2},{7,3},{8,12},{9,13},{10,... | collective-permute-start | bytes 786440 | tf_op jit(solution)/shard_map/ppermute | solution.py:35
  4.5 11.4 %collective-permute-start.8 = (bf16[512,256]{1,0:T(8,128)(2,1)}, bf16[512,256]{1,0:T(8,128)(2,1)S(1)}, u32[]{:S(2)}, u32[]{:S(2)}) collective-permute-start(bf16[512,256]{1,0:T(8,128)(2,1)} %bitcast.8), channel_id=1, source_target_pairs={{0,1},{1,0},{2,3},{3,2},{4,8},{5,9},{6,10},{7,11},{8,4},{9,5},{10,... | collective-permute-start | bytes 786440 | tf_op jit(solution)/shard_map/ppermute | solution.py:35
  12.4 8.3 %collective-permute-start.4 = (bf16[512,256]{1,0:T(8,128)(2,1)S(1)}, bf16[512,256]{1,0:T(8,128)(2,1)S(1)}, u32[]{:S(2)}, u32[]{:S(2)}) collective-permute-start(bf16[512,256]{1,0:T(8,128)(2,1)S(1)} %broadcast_select_fusion.1.refs_0_), channel_id=1, source_target_pairs={{2,0},{3,1},{0,2},{1,3},{6,4},{7,5},{4,6},{5,7},{10,8},{11,9},{8,1... | collective-permute-start | bytes 786440 | tf_op jit(solution)/shard_map/ppermute | solution.py:56
  16.0 8.5 %collective-permute-start.9 = (bf16[512,256]{1,0:T(8,128)(2,1)S(1)}, bf16[512,256]{1,0:T(8,128)(2,1)S(1)}, u32[]{:S(2)}, u32[]{:S(2)}) collective-permute-start(bf16[512,256]{1,0:T(8,128)(2,1)S(1)} %broadcast_select_fusion.refs_2_), channel_id=1, source_target_pairs={{2,0},{3,1},{0,2},{1,3},{6,4},{7,5},{4,6},{5,7},{10,8},{11,9},{8,1... | collective-permute-start | bytes 786440 | tf_op jit(solution)/shard_map/ppermute | solution.py:56
  17.6 9.3 %collective-permute-start.5 = (bf16[512,256]{1,0:T(8,128)(2,1)S(1)}, bf16[512,256]{1,0:T(8,128)(2,1)S(1)}, u32[]{:S(2)}, u32[]{:S(2)}) collective-permute-start(bf16[512,256]{1,0:T(8,128)(2,1)S(1)} %broadcast_select_fusion.1.refs_0_), channel_id=1, source_target_pairs={{1,0},{0,1},{3,2},{2,3},{5,4},{4,5},{7,6},{6,7},{9,8},{8,9},{11,10... | collective-permute-start | bytes 786440 | tf_op jit(solution)/shard_map/ppermute | solution.py:56
  20.7 6.1 %collective-permute-start.6 = (bf16[512,256]{1,0:T(8,128)(2,1)S(1)}, bf16[512,256]{1,0:T(8,128)(2,1)S(1)}, u32[]{:S(2)}, u32[]{:S(2)}) collective-permute-start(bf16[512,256]{1,0:T(8,128)(2,1)S(1)} %collective-permute-done.4.refs_1_), channel_id=1, source_target_pairs={{1,0},{0,1},{3,2},{2,3},{5,4},{4,5},{7,6},{6,7},{9,8},{8,9},{11,10... | collective-permute-start | bytes 786440 | tf_op jit(solution)/shard_map/ppermute | solution.py:56
  21.5 5.4 %collective-permute-start.1 = (f32[8,128]{1,0:T(8,128)S(1)}, f32[8,128]{1,0:T(8,128)S(1)}, u32[]{:S(2)}, u32[]{:S(2)}) collective-permute-start(f32[8,128]{1,0:T(8,128)S(1)} %shard_map.47), channel_id=1, source_target_pairs={{24,0},{28,4},{0,8},{4,12},{8,16},{12,20},{16,24},{20,28},{25,1},{... | collective-permute-start | bytes 12296 | tf_op jit(solution)/shard_map/ppermute | solution.py:25
  21.8 15.1 %collective-permute-start.10 = (bf16[512,256]{1,0:T(8,128)(2,1)S(1)}, bf16[512,256]{1,0:T(8,128)(2,1)S(1)}, u32[]{:S(2)}, u32[]{:S(2)}) collective-permute-start(bf16[512,256]{1,0:T(8,128)(2,1)S(1)} %broadcast_select_fusion.refs_2_), channel_id=1, source_target_pairs={{1,0},{0,1},{3,2},{2,3},{5,4},{4,5},{7,6},{6,7},{9,8},{8,9},{11,10... | collective-permute-start | bytes 786440 | tf_op jit(solution)/shard_map/ppermute | solution.py:56
  24.5 12.4 %collective-permute-start.11 = (bf16[512,256]{1,0:T(8,128)(2,1)S(1)}, bf16[512,256]{1,0:T(8,128)(2,1)S(1)}, u32[]{:S(2)}, u32[]{:S(2)}) collective-permute-start(bf16[512,256]{1,0:T(8,128)(2,1)S(1)} %collective-permute-done.9.refs_3_), channel_id=1, source_target_pairs={{1,0},{0,1},{3,2},{2,3},{5,4},{4,5},{7,6},{6,7},{9,8},{8,9},{11,10... | collective-permute-start | bytes 786440 | tf_op jit(solution)/shard_map/ppermute | solution.py:56
  26.9 2.1 %copy-start.1 = (s32[1,512]{1,0:T(1,128)S(1)}, s32[1,512]{1,0:T(1,128)}, u32[]{:S(2)}) copy-start(s32[1,512]{1,0:T(1,128)} %select_ref.1) | copy-start | bytes 6148
  26.9 2.3 %copy-start.2 = (bf16[1,512,256]{2,1,0:T(8,128)(2,1)S(1)}, bf16[1,512,256]{2,1,0:T(8,128)(2,1)}, u32[]{:S(2)}) copy-start(bf16[1,512,256]{2,1,0:T(8,128)(2,1)} %param.4) | copy-start | bytes 786436
  26.9 2.2 %copy-start = (f32[3,256]{1,0:T(4,128)S(1)}, f32[3,256]{1,0:T(4,128)}, u32[]{:S(2)}) copy-start(f32[3,256]{1,0:T(4,128)} %gain_ref.5) | copy-start | bytes 9220
  26.9 10.0 %collective-permute-start.12 = (bf16[512,256]{1,0:T(8,128)(2,1)S(1)}, bf16[512,256]{1,0:T(8,128)(2,1)S(1)}, u32[]{:S(2)}, u32[]{:S(2)}) collective-permute-start(bf16[512,256]{1,0:T(8,128)(2,1)S(1)} %shard_map.50), channel_id=1, source_target_pairs={{8,12},{12,16},{16,20},{20,24},{24,28},{0,8},{4,0},{28,4},{9,13},{... | collective-permute-start | bytes 786440 | tf_op jit(solution)/shard_map/ppermute | solution.py:234
  27.9 8.9 %collective-permute-start = (f32[8,128]{1,0:T(8,128)S(1)}, f32[8,128]{1,0:T(8,128)S(1)}, u32[]{:S(2)}, u32[]{:S(2)}) collective-permute-start(f32[8,128]{1,0:T(8,128)S(1)} %shard_map.47), channel_id=1, source_target_pairs={{28,0},{0,4},{4,8},{8,12},{12,16},{16,20},{20,24},{24,28},{29,1},{... | collective-permute-start | bytes 12296 | tf_op jit(solution)/shard_map/ppermute | solution.py:25

commit v7 on v6

--- a/solution.py
+++ b/solution.py
@@ -161,17 +161,36 @@
 
 
 def finish(
-    offset, section_ref, columns_ref, gain_ref, numerator_ref, count_ref, warped_ref, out_ref
+    offset,
+    section_ref,
+    columns_ref,
+    gain_ref,
+    numerator_ref,
+    count_ref,
+    warped_ref,
+    out_ref,
+    block_ref,
+    sems,
 ):
-    _, channels = warped_ref.shape
+    num_rows, channels = warped_ref.shape
     usable = is_usable(warped_ref)
     gain = gain_ref[offset - 1 : offset, :]
-    chosen = chosen_rows(columns_ref[...], offset, section_ref, usable)
-    divisor = jnp.maximum(count_ref[...] + chosen, 1.0)
-    numerator = numerator_ref[...] + (
-        warped_ref[...].astype(jnp.float32) * widen(chosen, channels) * gain
-    )
-    out_ref[...] = (numerator / widen(divisor, channels)).astype(jnp.bfloat16)
+    copies = []
+    for at, row in enumerate(range(0, num_rows, row_block)):
+        rows = slice(row, row + row_block)
+        chosen = chosen_rows(columns_ref[rows, :], offset, section_ref, usable)
+        divisor = jnp.maximum(count_ref[rows, :] + chosen, 1.0)
+        numerator = numerator_ref[rows, :] + (
+            warped_ref[rows, :].astype(jnp.float32) * widen(chosen, channels) * gain
+        )
+        block_ref[rows, :] = (numerator / widen(divisor, channels)).astype(jnp.bfloat16)
+        part = pl.ds(row, row_block)
+        copies.append(
+            pltpu.make_async_copy(block_ref.at[part, :], out_ref.at[part, :], sems.at[at])
+        )
+        copies[-1].start()
+    for copy in copies:
+        copy.wait()
 
 
 def shards(features, select, validity, offset_gain):
@@ -247,12 +266,19 @@
         heavy,
         1,
     )
-    out = call(
+    args = (section, columns, offset_gain, *state, third)
+    out = pl.pallas_call(
         functools.partial(finish, 3),
-        tile,
-        (section, columns, offset_gain, *state, third),
-        scalars=1,
-    )
+        out_shape=tile,
+        in_specs=[smem] + [vmem] * (len(args) - 1),
+        out_specs=pl.BlockSpec(memory_space=pl.ANY),
+        scratch_shapes=[
+            pltpu.VMEM((num_rows, channels), jnp.bfloat16),
+            pltpu.SemaphoreType.DMA((num_rows // row_block,)),
+        ],
+        compiler_params=grant,
+        name="finish",
+    )(*args)
     return out[None]
 
 

time: 38 us -> 37.9 us (level)
    pallas_call x6 -> x5, Pallas kernels: 1.23 us -> 0.35 us  [call(): pl.pallas_call(body, out_shape=out, in_specs=[smem] * scalars + [vmem] *...]
    pallas_call x0 -> x1, Pallas kernels: none -> 0.84 us  [shards(): pl.pallas_call(functools.partial(finish, 3), out_shape=tile, in_specs=[sm...]
where the time goes in v7:
time: 37.9 us; the launch traced here: 37.8 us
  waiting for transfers between devices  25.3 us (67%)
  starting transfers between devices  10.4 us (27%)
  Pallas kernels  1.2 us (3%)
  between operations  0.75 us (2%)
    ppermute x2, waiting for transfers between devices, from_behind(): lax.ppermute(block, 'sec', [((i - distance) % n, i) for i in range(n)])  10 us
    ppermute x4, waiting for transfers between devices, over_both(): return lax.ppermute(block, ('sec', 'tile'), pairs)  9.7 us
    ppermute x6, waiting for transfers between devices, from_partner(): return lax.ppermute(block, 'tile', [(i ^ distance, i) for i in range(n)])  5.61 us
    ppermute x4, starting transfers between devices, over_both(): return lax.ppermute(block, ('sec', 'tile'), pairs)  4.55 us
    ppermute x6, starting transfers between devices, from_partner(): return lax.ppermute(block, 'tile', [(i ^ distance, i) for i in range(n)])  3.49 us
    ppermute x2, starting transfers between devices, from_behind(): lax.ppermute(block, 'sec', [((i - distance) % n, i) for i in range(n)])  1.42 us
    ppermute x1, starting transfers between devices, shards(): third = lax.ppermute(answered, 'sec', routes)  0.99 us
    pallas_call x1, Pallas kernels, shards(): pl.pallas_call(functools.partial(finish, 3), out_shape=tile, in_specs=[sm...  0.84 us
  transfers between devices with their start and end apart: 13, of which 7 were waited for; matrix products, arithmetic and copies ran while one was open for 0% of the time, Pallas kernels for 1%

profile of v7, /device:TPU:0, one launch (start us, length us, event | category | flops | bytes accessed | tf_op | source)
XLA Modules:
  0.0 37.8 jit_solution(18337180491336424689)
XLA Ops:
  0.0 3.1 %collective-permute-start.2 = (bf16[512,256]{1,0:T(8,128)(2,1)}, bf16[512,256]{1,0:T(8,128)(2,1)S(1)}, u32[]{:S(2)}, u32[]{:S(2)}) collective-permute-start(bf16[512,256]{1,0:T(8,128)(2,1)} %bitcast.5), channel_id=1, source_target_pairs={{0,8},{1,0},{2,10},{3,2},{4,12},{5,4},{6,14},{7,6},{8,16},{9,1},{1... | collective-permute-start | bytes 786440 | tf_op jit(solution)/shard_map/ppermute | solution.py:35
  3.1 0.0 collective-permute-start.3
  3.1 1.5 %collective-permute-start.7 = (bf16[512,256]{1,0:T(8,128)(2,1)}, bf16[512,256]{1,0:T(8,128)(2,1)S(1)}, u32[]{:S(2)}, u32[]{:S(2)}) collective-permute-start(bf16[512,256]{1,0:T(8,128)(2,1)} %bitcast.7), channel_id=1, source_target_pairs={{0,4},{1,5},{2,6},{3,7},{4,0},{5,1},{6,2},{7,3},{8,12},{9,13},{10,... | collective-permute-start | bytes 786440 | tf_op jit(solution)/shard_map/ppermute | solution.py:35
  4.6 4.4 %collective-permute-done.2 = bf16[512,256]{1,0:T(8,128)(2,1)S(1)} collective-permute-done((bf16[512,256]{1,0:T(8,128)(2,1)}, bf16[512,256]{1,0:T(8,128)(2,1)S(1)}, u32[]{:S(2)}, u32[]{:S(2)}) %collective-permute-start.2) | collective-permute-done | bytes 262176 | tf_op jit(solution)/shard_map/ppermute | solution.py:35
  8.9 3.4 %collective-permute-done.3 = bf16[512,256]{1,0:T(8,128)(2,1)S(1)} collective-permute-done((bf16[512,256]{1,0:T(8,128)(2,1)}, bf16[512,256]{1,0:T(8,128)(2,1)S(1)}, u32[]{:S(2)}, u32[]{:S(2)}) %collective-permute-start.3) | collective-permute-done | bytes 262176 | tf_op jit(solution)/shard_map/ppermute | solution.py:35
  12.4 1.7 %collective-permute-start.4 = (bf16[512,256]{1,0:T(8,128)(2,1)S(1)}, bf16[512,256]{1,0:T(8,128)(2,1)S(1)}, u32[]{:S(2)}, u32[]{:S(2)}) collective-permute-start(bf16[512,256]{1,0:T(8,128)(2,1)S(1)} %broadcast_select_fusion.1.refs_0_), channel_id=1, source_target_pairs={{2,0},{3,1},{0,2},{1,3},{6,4},{7,5},{4,6},{5,7},{10,8},{11,9},{8,1... | collective-permute-start | bytes 786440 | tf_op jit(solution)/shard_map/ppermute | solution.py:56
  14.1 1.9 %collective-permute-done.7.beside_ref = bf16[512,256]{1,0:T(8,128)(2,1)S(1)} collective-permute-done((bf16[512,256]{1,0:T(8,128)(2,1)}, bf16[512,256]{1,0:T(8,128)(2,1)S(1)}, u32[]{:S(2)}, u32[]{:S(2)}) %collective-permute-start.7) | collective-permute-done | bytes 262176 | tf_op jit(solution)/shard_map/ppermute | solution.py:35
  15.9 0.0 collective-permute-done.8.across_ref
  16.0 1.6 %collective-permute-start.9 = (bf16[512,256]{1,0:T(8,128)(2,1)S(1)}, bf16[512,256]{1,0:T(8,128)(2,1)S(1)}, u32[]{:S(2)}, u32[]{:S(2)}) collective-permute-start(bf16[512,256]{1,0:T(8,128)(2,1)S(1)} %broadcast_select_fusion.refs_2_), channel_id=1, source_target_pairs={{2,0},{3,1},{0,2},{1,3},{6,4},{7,5},{4,6},{5,7},{10,8},{11,9},{8,1... | collective-permute-start | bytes 786440 | tf_op jit(solution)/shard_map/ppermute | solution.py:56
  17.6 3.2 %collective-permute-done.4.refs_1_ = bf16[512,256]{1,0:T(8,128)(2,1)S(1)} collective-permute-done((bf16[512,256]{1,0:T(8,128)(2,1)S(1)}, bf16[512,256]{1,0:T(8,128)(2,1)S(1)}, u32[]{:S(2)}, u32[]{:S(2)}) %collective-permute-start.4) | collective-permute-done | bytes 262176 | tf_op jit(solution)/shard_map/ppermute | solution.py:56
  21.4 0.1 shard_map.47
  21.5 0.3 collective-permute-start.1
  21.8 0.2 collective-permute-start.10
  22.0 2.4 %collective-permute-done.9.refs_3_ = bf16[512,256]{1,0:T(8,128)(2,1)S(1)} collective-permute-done((bf16[512,256]{1,0:T(8,128)(2,1)S(1)}, bf16[512,256]{1,0:T(8,128)(2,1)S(1)}, u32[]{:S(2)}, u32[]{:S(2)}) %collective-permute-start.9) | collective-permute-done | bytes 262176 | tf_op jit(solution)/shard_map/ppermute | solution.py:56
  24.5 2.4 %collective-permute-done.1.flag_ref = f32[8,128]{1,0:T(8,128)S(1)} collective-permute-done((f32[8,128]{1,0:T(8,128)S(1)}, f32[8,128]{1,0:T(8,128)S(1)}, u32[]{:S(2)}, u32[]{:S(2)}) %collective-permute-start.1) | collective-permute-done | bytes 4128 | tf_op jit(solution)/shard_map/ppermute | solution.py:25
  26.9 0.0 copy-start.2
  26.9 0.0 copy-start
  26.9 1.0 %collective-permute-start.12 = (bf16[512,256]{1,0:T(8,128)(2,1)S(1)}, bf16[512,256]{1,0:T(8,128)(2,1)S(1)}, u32[]{:S(2)}, u32[]{:S(2)}) collective-permute-start(bf16[512,256]{1,0:T(8,128)(2,1)S(1)} %shard_map.50), channel_id=1, source_target_pairs={{8,12},{12,16},{16,20},{20,24},{24,28},{0,8},{4,0},{28,4},{9,13},{... | collective-permute-start | bytes 786440 | tf_op jit(solution)/shard_map/ppermute | solution.py:253
  27.9 1.1 %collective-permute-start = (f32[8,128]{1,0:T(8,128)S(1)}, f32[8,128]{1,0:T(8,128)S(1)}, u32[]{:S(2)}, u32[]{:S(2)}) collective-permute-start(f32[8,128]{1,0:T(8,128)S(1)} %shard_map.47), channel_id=1, source_target_pairs={{28,0},{0,4},{4,8},{8,12},{12,16},{16,20},{20,24},{24,28},{29,1},{... | collective-permute-start | bytes 12296 | tf_op jit(solution)/shard_map/ppermute | solution.py:25
  29.0 0.1 shard_map.46.columns_ref
  29.2 0.1 shard_map.48
  29.3 7.6 %collective-permute-done.flag_ref = f32[8,128]{1,0:T(8,128)S(1)} collective-permute-done((f32[8,128]{1,0:T(8,128)S(1)}, f32[8,128]{1,0:T(8,128)S(1)}, u32[]{:S(2)}, u32[]{:S(2)}) %collective-permute-start) | collective-permute-done | bytes 4128 | tf_op jit(solution)/shard_map/ppermute | solution.py:25
  36.9 0.1 shard_map.49
  36.9 0.8 %finish.1 = bf16[512,256]{1,0:T(8,128)(2,1)} custom-call(s32[1]{0:T(128)} %bitcast.section_ref, s32[512,128]{1,0:T(8,128)S(1)} %shard_map.46.columns_ref, f32[3,256]{1,0:T(4,128)S(1)} %copy-done, f32[512,256]{1,0:T(8,128)S(1)} %get-tuple-element.11.numerator_ref, f32[512,128]{1,0:T(8,128)S(1)} %get-tuple-element.12.count_ref, ...), custom_call_target="tpu_custom_call" | custom-call | tf_op jit(solution)/shard_map/finish/pallas_call | solution.py:270
  (16 shorter events, 0.1 us)
Async XLA Ops:
  0.0 8.9 %collective-permute-start.2 = (bf16[512,256]{1,0:T(8,128)(2,1)}, bf16[512,256]{1,0:T(8,128)(2,1)S(1)}, u32[]{:S(2)}, u32[]{:S(2)}) collective-permute-start(bf16[512,256]{1,0:T(8,128)(2,1)} %bitcast.5), channel_id=1, source_target_pairs={{0,8},{1,0},{2,10},{3,2},{4,12},{5,4},{6,14},{7,6},{8,16},{9,1},{1... | collective-permute-start | bytes 786440 | tf_op jit(solution)/shard_map/ppermute | solution.py:35
  3.1 9.3 %collective-permute-start.3 = (bf16[512,256]{1,0:T(8,128)(2,1)}, bf16[512,256]{1,0:T(8,128)(2,1)S(1)}, u32[]{:S(2)}, u32[]{:S(2)}) collective-permute-start(bf16[512,256]{1,0:T(8,128)(2,1)} %bitcast.6), channel_id=1, source_target_pairs={{0,1},{1,9},{2,3},{3,11},{4,5},{5,13},{6,7},{7,15},{8,0},{9,17},{1... | collective-permute-start | bytes 786440 | tf_op jit(solution)/shard_map/ppermute | solution.py:35
  3.1 12.9 %collective-permute-start.7 = (bf16[512,256]{1,0:T(8,128)(2,1)}, bf16[512,256]{1,0:T(8,128)(2,1)S(1)}, u32[]{:S(2)}, u32[]{:S(2)}) collective-permute-start(bf16[512,256]{1,0:T(8,128)(2,1)} %bitcast.7), channel_id=1, source_target_pairs={{0,4},{1,5},{2,6},{3,7},{4,0},{5,1},{6,2},{7,3},{8,12},{9,13},{10,... | collective-permute-start | bytes 786440 | tf_op jit(solution)/shard_map/ppermute | solution.py:35
  4.5 11.4 %collective-permute-start.8 = (bf16[512,256]{1,0:T(8,128)(2,1)}, bf16[512,256]{1,0:T(8,128)(2,1)S(1)}, u32[]{:S(2)}, u32[]{:S(2)}) collective-permute-start(bf16[512,256]{1,0:T(8,128)(2,1)} %bitcast.8), channel_id=1, source_target_pairs={{0,1},{1,0},{2,3},{3,2},{4,8},{5,9},{6,10},{7,11},{8,4},{9,5},{10,... | collective-permute-start | bytes 786440 | tf_op jit(solution)/shard_map/ppermute | solution.py:35
  12.4 8.3 %collective-permute-start.4 = (bf16[512,256]{1,0:T(8,128)(2,1)S(1)}, bf16[512,256]{1,0:T(8,128)(2,1)S(1)}, u32[]{:S(2)}, u32[]{:S(2)}) collective-permute-start(bf16[512,256]{1,0:T(8,128)(2,1)S(1)} %broadcast_select_fusion.1.refs_0_), channel_id=1, source_target_pairs={{2,0},{3,1},{0,2},{1,3},{6,4},{7,5},{4,6},{5,7},{10,8},{11,9},{8,1... | collective-permute-start | bytes 786440 | tf_op jit(solution)/shard_map/ppermute | solution.py:56
  16.0 8.5 %collective-permute-start.9 = (bf16[512,256]{1,0:T(8,128)(2,1)S(1)}, bf16[512,256]{1,0:T(8,128)(2,1)S(1)}, u32[]{:S(2)}, u32[]{:S(2)}) collective-permute-start(bf16[512,256]{1,0:T(8,128)(2,1)S(1)} %broadcast_select_fusion.refs_2_), channel_id=1, source_target_pairs={{2,0},{3,1},{0,2},{1,3},{6,4},{7,5},{4,6},{5,7},{10,8},{11,9},{8,1... | collective-permute-start | bytes 786440 | tf_op jit(solution)/shard_map/ppermute | solution.py:56
  17.6 9.3 %collective-permute-start.5 = (bf16[512,256]{1,0:T(8,128)(2,1)S(1)}, bf16[512,256]{1,0:T(8,128)(2,1)S(1)}, u32[]{:S(2)}, u32[]{:S(2)}) collective-permute-start(bf16[512,256]{1,0:T(8,128)(2,1)S(1)} %broadcast_select_fusion.1.refs_0_), channel_id=1, source_target_pairs={{1,0},{0,1},{3,2},{2,3},{5,4},{4,5},{7,6},{6,7},{9,8},{8,9},{11,10... | collective-permute-start | bytes 786440 | tf_op jit(solution)/shard_map/ppermute | solution.py:56
  20.7 6.1 %collective-permute-start.6 = (bf16[512,256]{1,0:T(8,128)(2,1)S(1)}, bf16[512,256]{1,0:T(8,128)(2,1)S(1)}, u32[]{:S(2)}, u32[]{:S(2)}) collective-permute-start(bf16[512,256]{1,0:T(8,128)(2,1)S(1)} %collective-permute-done.4.refs_1_), channel_id=1, source_target_pairs={{1,0},{0,1},{3,2},{2,3},{5,4},{4,5},{7,6},{6,7},{9,8},{8,9},{11,10... | collective-permute-start | bytes 786440 | tf_op jit(solution)/shard_map/ppermute | solution.py:56
  21.5 5.4 %collective-permute-start.1 = (f32[8,128]{1,0:T(8,128)S(1)}, f32[8,128]{1,0:T(8,128)S(1)}, u32[]{:S(2)}, u32[]{:S(2)}) collective-permute-start(f32[8,128]{1,0:T(8,128)S(1)} %shard_map.47), channel_id=1, source_target_pairs={{24,0},{28,4},{0,8},{4,12},{8,16},{12,20},{16,24},{20,28},{25,1},{... | collective-permute-start | bytes 12296 | tf_op jit(solution)/shard_map/ppermute | solution.py:25
  21.8 15.1 %collective-permute-start.10 = (bf16[512,256]{1,0:T(8,128)(2,1)S(1)}, bf16[512,256]{1,0:T(8,128)(2,1)S(1)}, u32[]{:S(2)}, u32[]{:S(2)}) collective-permute-start(bf16[512,256]{1,0:T(8,128)(2,1)S(1)} %broadcast_select_fusion.refs_2_), channel_id=1, source_target_pairs={{1,0},{0,1},{3,2},{2,3},{5,4},{4,5},{7,6},{6,7},{9,8},{8,9},{11,10... | collective-permute-start | bytes 786440 | tf_op jit(solution)/shard_map/ppermute | solution.py:56
  24.5 12.4 %collective-permute-start.11 = (bf16[512,256]{1,0:T(8,128)(2,1)S(1)}, bf16[512,256]{1,0:T(8,128)(2,1)S(1)}, u32[]{:S(2)}, u32[]{:S(2)}) collective-permute-start(bf16[512,256]{1,0:T(8,128)(2,1)S(1)} %collective-permute-done.9.refs_3_), channel_id=1, source_target_pairs={{1,0},{0,1},{3,2},{2,3},{5,4},{4,5},{7,6},{6,7},{9,8},{8,9},{11,10... | collective-permute-start | bytes 786440 | tf_op jit(solution)/shard_map/ppermute | solution.py:56
  26.9 2.1 %copy-start.1 = (s32[1,512]{1,0:T(1,128)S(1)}, s32[1,512]{1,0:T(1,128)}, u32[]{:S(2)}) copy-start(s32[1,512]{1,0:T(1,128)} %select_ref.1) | copy-start | bytes 6148
  26.9 2.3 %copy-start.2 = (bf16[1,512,256]{2,1,0:T(8,128)(2,1)S(1)}, bf16[1,512,256]{2,1,0:T(8,128)(2,1)}, u32[]{:S(2)}) copy-start(bf16[1,512,256]{2,1,0:T(8,128)(2,1)} %param.4) | copy-start | bytes 786436
  26.9 2.2 %copy-start = (f32[3,256]{1,0:T(4,128)S(1)}, f32[3,256]{1,0:T(4,128)}, u32[]{:S(2)}) copy-start(f32[3,256]{1,0:T(4,128)} %gain_ref.5) | copy-start | bytes 9220
  26.9 10.0 %collective-permute-start.12 = (bf16[512,256]{1,0:T(8,128)(2,1)S(1)}, bf16[512,256]{1,0:T(8,128)(2,1)S(1)}, u32[]{:S(2)}, u32[]{:S(2)}) collective-permute-start(bf16[512,256]{1,0:T(8,128)(2,1)S(1)} %shard_map.50), channel_id=1, source_target_pairs={{8,12},{12,16},{16,20},{20,24},{24,28},{0,8},{4,0},{28,4},{9,13},{... | collective-permute-start | bytes 786440 | tf_op jit(solution)/shard_map/ppermute | solution.py:253
  27.9 8.9 %collective-permute-start = (f32[8,128]{1,0:T(8,128)S(1)}, f32[8,128]{1,0:T(8,128)S(1)}, u32[]{:S(2)}, u32[]{:S(2)}) collective-permute-start(f32[8,128]{1,0:T(8,128)S(1)} %shard_map.47), channel_id=1, source_target_pairs={{28,0},{0,4},{4,8},{8,12},{12,16},{16,20},{20,24},{24,28},{29,1},{... | collective-permute-start | bytes 12296 | tf_op jit(solution)/shard_map/ppermute | solution.py:25
